TPU v7x, 32 devices: a whole 2x2x4 slice. The times are simulated.
32 devices in a mesh: fsdp: 32 (over z, y, x, core).
Axes of the slice: x: 2, y: 2, z: 4, core: 2. Of those that a mesh axis runs over, the one named last changes fastest.
Arguments:
- layer_input: bfloat16 [96, 288, 768], P('fsdp'), may hold values from -6 to 6
- segments: int32 [96, 288], P('fsdp'), may hold values from 0 to 8, as said below
- cotangent: bfloat16 [96, 288, 768], P('fsdp'), may hold values from -6 to 6
- pre_gain: float32 [768], P('fsdp'), may hold values from 0.5 to 1.5
- pre_shift: float32 [768], P('fsdp'), may hold values from -2 to 2
- w_qkv: float32 [768, 2304], P('fsdp'), may hold values from -0.21875 to 0.21875
- b_query: float32 [768], P('fsdp'), may hold values from -3 to 3
- b_value: float32 [768], P('fsdp'), may hold values from -3 to 3
- w_out: float32 [768, 768], P('fsdp'), may hold values from -1.25 to 1.25
- b_out: float32 [768], P('fsdp'), may hold values from -3 to 3
- mid_gain: float32 [768], P('fsdp'), may hold values from 0.5 to 1.5
- mid_shift: float32 [768], P('fsdp'), may hold values from -2 to 2
- w_up: float32 [768, 3072], P('fsdp'), may hold values from -0.21875 to 0.21875
- b_up: float32 [3072], P('fsdp'), may hold values from -3 to 3
- w_down: float32 [3072, 768], P('fsdp'), may hold values from -0.109375 to 0.109375
- b_down: float32 [768], P('fsdp'), may hold values from -3 to 3
Outputs:
- layer_output: bfloat16 [96, 288, 768], P('fsdp')
- grad_input: bfloat16 [96, 288, 768], P('fsdp')
- grad_pre_gain: float32 [768], P('fsdp')
- grad_pre_shift: float32 [768], P('fsdp')
- grad_w_qkv: float32 [768, 2304], P('fsdp')
- grad_b_query: float32 [768], P('fsdp')
- grad_b_value: float32 [768], P('fsdp')
- grad_w_out: float32 [768, 768], P('fsdp')
- grad_b_out: float32 [768], P('fsdp')
- grad_mid_gain: float32 [768], P('fsdp')
- grad_mid_shift: float32 [768], P('fsdp')
- grad_w_up: float32 [768, 3072], P('fsdp')
- grad_b_up: float32 [3072], P('fsdp')
- grad_w_down: float32 [3072, 768], P('fsdp')
- grad_b_down: float32 [768], P('fsdp')
Inputs may be any that keep to these rules, and one draw needn't show every extreme that they name: `segments`: each row holds 8 or 7 images of 36 slots each, in slot order and numbered from 1; the remaining slots of a row are padding (0).
All inputs are finite; a program needn't handle non-finite values.
Results may differ from a plain program's by a relative error of at most 0.012.
The roundings to bfloat16 on the way count: a program that leaves them out, or rounds other values in their place, can miss the bound.
Values may be sent and summed in bfloat16 or wider, within the bound.
No kernel may reach another device: no remote copies, remote signals or barrier semaphores. Data moves between devices by JAX's collectives and lax.ppermute only.
A program may use at most 192 MiB of HBM per device.

v0:
```python
import jax
import jax.numpy as jnp
from jax import lax
from jax.experimental import pallas as pl
from jax.experimental.pallas import tpu as pltpu
from jax.sharding import PartitionSpec as P

HEAD_DIM = 64
PAIR = 2 * HEAD_DIM
LANES = 128
EPSILON = 1e-06
BLOCKED = -1e9
AXIS = "fsdp"
FF_TILE = 384
VMEM_LIMIT = 60 << 20
F32 = jnp.float32
BF16 = jnp.bfloat16


def wide(value):
    return value.astype(F32)


def low(value):
    return value.astype(BF16)


def dot(left, right, left_dim=1, right_dim=0):
    return lax.dot_general(
        left, right, (((left_dim,), (right_dim,)), ((), ())), preferred_element_type=F32
    )


def axes_of(count):
    rest = count.bit_length() - 2
    side = rest // 3
    return (1 << side, 1), (1 << side, 1 + side), (1 << (rest - 2 * side), 1 + 2 * side)


def swap(value, mask, count):
    return lax.ppermute(value, AXIS, [(i, i ^ mask) for i in range(count)])


def my_id():
    return lax.axis_index(AXIS).astype(jnp.int32)[None]


def gather(value, axis, count):
    size, bit = axis
    return [value] + [swap(value, d << bit, count) for d in range(1, size)]


def gather_chips(shard, count):
    x, y, z = axes_of(count)
    column = jnp.stack(gather(shard, z, count))
    half = z[0] // 2
    left = jnp.stack(gather(column[:half], x, count))
    right = jnp.stack(gather(column[half:], y, count))
    return gather(left, y, count) + gather(right, x, count)


def gather_core(pieces, count):
    return pieces + [swap(piece, 1, count) for piece in pieces]


def lay_out(pieces, count):
    (xs, xbit), (ys, ybit), (zs, zbit) = axes_of(count)
    block = pieces[0].shape[2:]
    half = zs // 2

    def body(id_ref, *refs):
        sources, out, sems = refs[: len(pieces)], refs[-2], refs[-1]
        copies = []
        for index, source in enumerate(sources):
            c, place = divmod(index, ys + xs)
            for inner in range(source.shape[0]):
                for m in range(half):
                    if place < ys:
                        block_id = c | inner << xbit | place << ybit | m << zbit
                    else:
                        block_id = c | (place - ys) << xbit | inner << ybit | (m + half) << zbit
                    copy = pltpu.make_async_copy(
                        source.at[inner, m], out.at[id_ref[0] ^ block_id], sems.at[len(copies)]
                    )
                    copy.start()
                    copies.append(copy)
        for copy in copies:
            copy.wait()

    full = pl.pallas_call(
        body,
        out_shape=jax.ShapeDtypeStruct((count,) + block, pieces[0].dtype),
        in_specs=[pl.BlockSpec(memory_space=pltpu.SMEM)]
        + [pl.BlockSpec(memory_space=pl.ANY)] * len(pieces),
        out_specs=pl.BlockSpec(memory_space=pltpu.VMEM),
        scratch_shapes=[pltpu.SemaphoreType.DMA((count,))],
        name="lay_out",
    )(my_id(), *pieces)
    return full.reshape((count * block[0],) + block[1:])


def reduce_axis(parts, axis, count):
    size, bit = axis
    total = wide(parts[0])
    for d in range(1, size):
        total = total + wide(swap(parts[d], d << bit, count))
    return total


def reduce_blocks(keep, send, count):
    x, y, z = axes_of(count)
    shape = (z[0], y[0], x[0]) + keep.shape[1:]
    both = wide(keep) + wide(swap(send, 1, count))
    both = low(both).reshape(shape)
    half = z[0] // 2
    left = [both[:half, :, d] for d in range(x[0])]
    left = low(reduce_axis(left, x, count))
    right = [both[half:, d] for d in range(y[0])]
    right = low(reduce_axis(right, y, count))
    left = low(reduce_axis([left[:, d] for d in range(y[0])], y, count))
    right = low(reduce_axis([right[:, d] for d in range(x[0])], x, count))
    column = [left[m] for m in range(half)] + [right[m] for m in range(half)]
    return reduce_axis(column, z, count)


def same(rows, columns, shift, period):
    row = lax.broadcasted_iota(jnp.int32, (rows, columns), 0)
    column = lax.broadcasted_iota(jnp.int32, (rows, columns), 1)
    return row == shift + column % period


def owned(count, columns, share):
    row = lax.broadcasted_iota(jnp.int32, (count, columns), 0)
    column = lax.broadcasted_iota(jnp.int32, (count, columns), 1)
    return row == column // share


def pack_near(qkv, out, vectors):
    rows = qkv.shape[0]
    sizes = [vector.shape[0] for vector in vectors]
    used = -(-sum(sizes) // LANES)
    columns = qkv.shape[1] + out.shape[1] + LANES

    def body(qkv_ref, out_ref, *refs):
        near_ref = refs[-1]
        near_ref[:, : qkv.shape[1]] = low(qkv_ref[...])
        near_ref[:, qkv.shape[1] : columns - LANES] = low(out_ref[...])
        number = lax.broadcasted_iota(jnp.int32, (rows, LANES), 0)
        block = jnp.zeros((rows, LANES), F32)
        for line in range(used):
            text, start = jnp.zeros((8, LANES), F32), 0
            for ref, size in zip(refs, sizes):
                if start < (line + 1) * LANES and start + size > line * LANES:
                    column = lax.broadcasted_iota(jnp.int32, (size, LANES), 1)
                    row = lax.broadcasted_iota(jnp.int32, (size, LANES), 0)
                    pick = low((column == row + (start - line * LANES)).astype(F32))
                    text = text + dot(low(jnp.broadcast_to(ref[...], (8, size))), pick)
                start += size
            block = jnp.where(number == line, text[:1], block)
        near_ref[:, columns - LANES :] = low(block)

    vmem = pl.BlockSpec(memory_space=pltpu.VMEM)
    return pl.pallas_call(
        body,
        out_shape=jax.ShapeDtypeStruct((rows, columns), BF16),
        in_specs=[vmem] * (2 + len(vectors)),
        out_specs=vmem,
        name="pack_near",
    )(qkv, out, *[vector.reshape(1, -1) for vector in vectors])


def unpack_small(weights, count, width, wider):
    rows = width // count
    share, long_share = rows, wider // count
    used = -(-(8 * share + long_share) // LANES)

    def body(block_ref, vectors_ref, long_ref):
        block = wide(block_ref[...]).reshape(count, rows, LANES)
        flat = [low(block[:, line, :]) for line in range(used)]

        def spread(shift, period, columns):
            total = jnp.zeros((count, columns), F32)
            for line in range(used):
                pick = same(LANES, columns, shift - line * LANES, period)
                total = total + dot(flat[line], low(pick.astype(F32)))
            mine = jnp.where(owned(count, columns, period), total, 0.0)
            return jnp.sum(mine, axis=0, keepdims=True)

        for v in range(8):
            vectors_ref[v : v + 1, :] = spread(v * share, share, width)
        long_ref[...] = spread(8 * share, long_share, wider)

    return pl.pallas_call(
        body,
        grid=(1,),
        out_shape=(jax.ShapeDtypeStruct((8, width), F32), jax.ShapeDtypeStruct((1, wider), F32)),
        in_specs=[pl.BlockSpec((width, LANES), lambda i: (0, weights.shape[1] // LANES - 1))],
        out_specs=(
            pl.BlockSpec((8, width), lambda i: (0, 0)),
            pl.BlockSpec((1, wider), lambda i: (0, 0)),
        ),
        name="unpack_small",
    )(weights)


def normalized(value):
    centred = value - jnp.mean(value, axis=-1, keepdims=True)
    scale = lax.rsqrt(jnp.mean(centred * centred, axis=-1, keepdims=True) + EPSILON)
    return centred * scale, scale


def norm_back(grad, unit, scale, gain):
    inner = grad * gain
    average = jnp.mean(inner, axis=-1, keepdims=True)
    along = jnp.mean(inner * unit, axis=-1, keepdims=True)
    return scale * (inner - average - unit * along)


def column_sums(value):
    return jnp.sum(value, axis=0, keepdims=True)


def halves():
    lane = lax.broadcasted_iota(jnp.int32, (1, PAIR), 1)
    first = low((lane < HEAD_DIM).astype(F32))
    return first, low((lane >= HEAD_DIM).astype(F32))


def mask_of(across, down):
    slots = across.shape[1]
    row = lax.broadcasted_iota(jnp.int32, (slots, slots), 0)
    column = lax.broadcasted_iota(jnp.int32, (slots, slots), 1)
    allowed = ((down == across) & (down > 0)) | (row == column)
    return jnp.where(allowed, 0.0, BLOCKED)


def spread(product, rows, count, me, keep, send):
    if rows % 8 == 0:

        def place(slot, carry):
            for c, out in enumerate((keep, send)):
                start = pl.multiple_of((me ^ (2 * slot + c)) * rows, 8)
                out[slot] = low(product[pl.ds(start, rows), :])
            return carry

        lax.fori_loop(0, count // 2, place, 0)
        return
    for couple in range(count // 2):
        slot = couple ^ (me // 2)
        even = low(product[2 * couple * rows : (2 * couple + 1) * rows, :])
        odd = low(product[(2 * couple + 1) * rows : (2 * couple + 2) * rows, :])
        keep[slot] = jnp.where(me % 2 == 0, even, odd)
        send[slot] = jnp.where(me % 2 == 0, odd, even)


def attend(x, across, down, weights, vectors):
    tokens, width = x.shape
    slots = across.shape[2]
    rows = tokens // slots
    heads = width // HEAD_DIM

    def body(x_ref, across_ref, down_ref, w_ref, vec_ref, first_ref, qkv_ref, ctx_ref, lse_ref, mid_ref, second_ref):
        value = wide(x_ref[...])
        unit, _ = normalized(value)
        first = low(unit * vec_ref[0:1, :] + vec_ref[1:2, :])
        first_ref[...] = first
        for part in range(3):
            product = dot(first, w_ref[:, part * width : (part + 1) * width])
            if part != 1:
                product = product + vec_ref[2 + part // 2 : 3 + part // 2, :]
            qkv_ref[:, part * width : (part + 1) * width] = low(product)
        bias = mask_of(across_ref[0], down_ref[...])
        masks = halves()
        for pair in range(heads // 2):
            lanes = slice(pair * PAIR, (pair + 1) * PAIR)
            q = qkv_ref[:, lanes]
            k = qkv_ref[:, width + pair * PAIR : width + (pair + 1) * PAIR]
            v = qkv_ref[:, 2 * width + pair * PAIR : 2 * width + (pair + 1) * PAIR]
            context = jnp.zeros((slots, PAIR), F32)
            for side in range(2):
                scores = dot(q * masks[side], k, 1, 1) * HEAD_DIM**-0.5 + bias
                highest = jnp.max(scores, axis=-1, keepdims=True)
                powers = jnp.exp(scores - highest)
                total = jnp.sum(powers, axis=-1, keepdims=True)
                probs = low(powers * (1.0 / total))
                context = context + dot(probs, v * masks[side])
                head = 2 * pair + side
                lse_ref[:, head : head + 1] = highest + jnp.log(total)
            ctx_ref[:, lanes] = low(context)
        attention = dot(ctx_ref[...], w_ref[:, 3 * width : 4 * width]) + vec_ref[4:5, :]
        middle = value + attention
        mid_ref[...] = middle
        unit, _ = normalized(middle)
        second_ref[...] = low(unit * vec_ref[5:6, :] + vec_ref[6:7, :])

    def row(columns):
        return pl.BlockSpec((slots, columns), lambda i: (i, 0))

    def whole(array):
        return pl.BlockSpec(array.shape, lambda i: (0, 0), pipeline_mode=pl.Buffered(1))

    shapes = [(width, BF16), (3 * width, BF16), (width, BF16), (heads, F32), (width, F32), (width, BF16)]
    return pl.pallas_call(
        body,
        grid=(rows,),
        out_shape=tuple(jax.ShapeDtypeStruct((tokens, c), t) for c, t in shapes),
        in_specs=[
            row(width),
            pl.BlockSpec((1, 1, slots), lambda i: (i, 0, 0)),
            row(1),
            whole(weights),
            whole(vectors),
        ],
        out_specs=tuple(row(c) for c, _ in shapes),
        compiler_params=pltpu.CompilerParams(vmem_limit_bytes=VMEM_LIMIT),
        cost_estimate=pl.CostEstimate(
            flops=2 * tokens * width * width * 4 + 4 * rows * heads * slots * slots * HEAD_DIM,
            transcendentals=rows * heads * slots * slots,
            bytes_accessed=30 << 20,
        ),
        name="attend",
    )(x, across, down, weights, vectors)


def feed_forward(second, upstream, middle, up, down, vectors, long_bias, count):
    tokens, width = second.shape
    wider = up.shape[1]
    tile = FF_TILE
    steps = wider // tile
    down_rows = wider // count
    group = tile // down_rows

    def body(
        id_ref, second_ref, grad_ref, mid_ref, up_ref, down_ref, vec_ref, bias_ref,
        out_ref, back_ref, down_keep, down_send, long_ref, rows_ref,
        out_sum, down_product,
    ):
        step = pl.program_id(0)
        me = id_ref[0]

        @pl.when(step == 0)
        def _():
            out_sum[...] = jnp.zeros_like(out_sum)

        grads = grad_ref[...]
        hidden = dot(second_ref[...], up_ref[...]) + bias_ref[...]
        below = 0.5 * (1.0 + lax.erf(hidden * 0.7071067811865476))
        active = low(hidden * below)
        slope = below + hidden * (jnp.exp(hidden * hidden * -0.5) * 0.3989422804014327)
        back = low(dot(grads, down_ref[...], 1, 1) * slope)
        back_ref[...] = back
        long_ref[...] = column_sums(wide(back))
        out_sum[...] += dot(active, down_ref[...])
        down_product[...] = dot(active, grads, 0, 0)
        spread(down_product, down_rows, group, me % group, down_keep, down_send)

        @pl.when(step == steps - 1)
        def _():
            out_ref[...] = low(mid_ref[...] + (out_sum[...] + vec_ref[7:8, :]))
            rows_ref[...] = jnp.broadcast_to(column_sums(wide(grads)), (8, width))

    def whole(array):
        return pl.BlockSpec(array.shape, lambda i, m: (0, 0), pipeline_mode=pl.Buffered(1))

    half = count // 2
    down_spec = pl.BlockSpec((group // 2, down_rows, width), lambda i, m: (i ^ (m[0] // group), 0, 0))
    return pl.pallas_call(
        body,
        grid_spec=pltpu.PrefetchScalarGridSpec(
            num_scalar_prefetch=1,
            grid=(steps,),
            in_specs=[
                whole(second), whole(upstream), whole(middle),
                pl.BlockSpec((width, tile), lambda i, m: (0, i)),
                pl.BlockSpec((tile, width), lambda i, m: (i, 0)),
                whole(vectors),
                pl.BlockSpec((1, tile), lambda i, m: (0, i)),
            ],
            out_specs=(
                pl.BlockSpec((tokens, width), lambda i, m: (0, 0)),
                pl.BlockSpec((tokens, tile), lambda i, m: (0, i)),
                down_spec, down_spec,
                pl.BlockSpec((1, tile), lambda i, m: (0, i)),
                pl.BlockSpec((8, width), lambda i, m: (0, 0)),
            ),
            scratch_shapes=[pltpu.VMEM((tokens, width), F32), pltpu.VMEM((tile, width), F32)],
        ),
        out_shape=(
            jax.ShapeDtypeStruct((tokens, width), BF16),
            jax.ShapeDtypeStruct((tokens, wider), BF16),
            jax.ShapeDtypeStruct((half, down_rows, width), BF16),
            jax.ShapeDtypeStruct((half, down_rows, width), BF16),
            jax.ShapeDtypeStruct((1, wider), F32),
            jax.ShapeDtypeStruct((8, width), F32),
        ),
        compiler_params=pltpu.CompilerParams(vmem_limit_bytes=VMEM_LIMIT),
        cost_estimate=pl.CostEstimate(
            flops=8 * tokens * width * wider, transcendentals=2 * tokens * wider,
            bytes_accessed=30 << 20,
        ),
        name="feed_forward",
    )(my_id(), second, upstream, middle, up, down, vectors, long_bias)


def feed_back(second, back, upstream, middle, up, vectors, count):
    tokens, width = second.shape
    wider = up.shape[1]
    tile = FF_TILE
    steps = wider // tile
    up_rows = width // count

    def body(
        id_ref, second_ref, back_ref, grad_ref, mid_ref, up_ref, vec_ref,
        dmid_ref, up_keep, up_send, rows_ref,
        back_sum, second_turned, up_product,
    ):
        step = pl.program_id(0)

        @pl.when(step == 0)
        def _():
            second_turned[...] = second_ref[...].T
            back_sum[...] = jnp.zeros_like(back_sum)

        back_sum[...] += dot(back_ref[...], up_ref[...], 1, 1)
        up_product[...] = dot(second_turned[...], back_ref[...])
        spread(up_product, up_rows, count, id_ref[0], up_keep, up_send)

        @pl.when(step == steps - 1)
        def _():
            unit, scale = normalized(mid_ref[...])
            da = back_sum[...]
            dmid_ref[...] = wide(grad_ref[...]) + norm_back(da, unit, scale, vec_ref[5:6, :])
            rows_ref[...] = jnp.zeros_like(rows_ref)
            rows_ref[0:1, :] = column_sums(da * unit)
            rows_ref[1:2, :] = column_sums(da)

    def whole(array):
        return pl.BlockSpec(array.shape, lambda i, m: (0, 0), pipeline_mode=pl.Buffered(1))

    half = count // 2
    up_spec = pl.BlockSpec((half, up_rows, tile), lambda i, m: (0, 0, i))
    return pl.pallas_call(
        body,
        grid_spec=pltpu.PrefetchScalarGridSpec(
            num_scalar_prefetch=1,
            grid=(steps,),
            in_specs=[
                whole(second),
                pl.BlockSpec((tokens, tile), lambda i, m: (0, i)),
                whole(upstream), whole(middle),
                pl.BlockSpec((width, tile), lambda i, m: (0, i)),
                whole(vectors),
            ],
            out_specs=(
                pl.BlockSpec((tokens, width), lambda i, m: (0, 0)),
                up_spec, up_spec,
                pl.BlockSpec((8, width), lambda i, m: (0, 0)),
            ),
            scratch_shapes=[
                pltpu.VMEM((tokens, width), F32), pltpu.VMEM((width, tokens), BF16),
                pltpu.VMEM((width, tile), F32),
            ],
        ),
        out_shape=(
            jax.ShapeDtypeStruct((tokens, width), F32),
            jax.ShapeDtypeStruct((half, up_rows, wider), BF16),
            jax.ShapeDtypeStruct((half, up_rows, wider), BF16),
            jax.ShapeDtypeStruct((8, width), F32),
        ),
        compiler_params=pltpu.CompilerParams(vmem_limit_bytes=VMEM_LIMIT),
        cost_estimate=pl.CostEstimate(
            flops=4 * tokens * width * wider, transcendentals=tokens, bytes_accessed=25 << 20
        ),
        name="feed_back",
    )(my_id(), second, back, upstream, middle, up, vectors)


def attend_back(x, across, down, weights, vectors, qkv, lse, dmid):
    tokens, width = x.shape
    slots = across.shape[2]
    rows = tokens // slots
    heads = width // HEAD_DIM

    def body(
        x_ref, across_ref, down_ref, w_ref, vec_ref, qkv_ref, lse_ref, dmid_ref,
        dx_ref, dqkv_ref, dattn_ref, sums,
        dctx,
    ):
        @pl.when(pl.program_id(0) == 0)
        def _():
            sums[...] = jnp.zeros_like(sums)

        middle_grad = dmid_ref[...]
        dattn = low(middle_grad)
        dattn_ref[...] = dattn
        dctx[...] = low(dot(dattn, w_ref[:, 3 * width : 4 * width], 1, 1))
        bias = mask_of(across_ref[0], down_ref[...])
        masks = halves()
        for pair in range(heads // 2):
            lanes = [slice(p * width + pair * PAIR, p * width + (pair + 1) * PAIR) for p in range(3)]
            q, k, v = (qkv_ref[:, lane] for lane in lanes)
            dout = dctx[:, lanes[0]]
            dq = jnp.zeros((slots, PAIR), F32)
            dk = jnp.zeros((slots, PAIR), F32)
            dv = jnp.zeros((slots, PAIR), F32)
            for side in range(2):
                head = 2 * pair + side
                q_half, dout_half = q * masks[side], dout * masks[side]
                scores = dot(q_half, k, 1, 1) * HEAD_DIM**-0.5 + bias
                probs = jnp.exp(scores - lse_ref[:, head : head + 1])
                dprobs = dot(dout_half, v, 1, 1)
                weighted = probs * dprobs
                dscores = low(weighted - probs * jnp.sum(weighted, axis=-1, keepdims=True))
                dv = dv + dot(low(probs), dout_half, 0, 0)
                dq = dq + dot(dscores, k * masks[side])
                dk = dk + dot(dscores, q_half, 0, 0)
            dqkv_ref[:, lanes[0]] = low(dq * HEAD_DIM**-0.5)
            dqkv_ref[:, lanes[1]] = low(dk * HEAD_DIM**-0.5)
            dqkv_ref[:, lanes[2]] = low(dv)
        dfirst = jnp.zeros((slots, width), F32)
        for p in range(3):
            part = slice(p * width, (p + 1) * width)
            dfirst = dfirst + dot(dqkv_ref[:, part], w_ref[:, part], 1, 1)
        unit, scale = normalized(wide(x_ref[...]))
        dx_ref[...] = low(middle_grad + norm_back(dfirst, unit, scale, vec_ref[0:1, :]))
        sums[0:1, :] += column_sums(dfirst * unit)
        sums[1:2, :] += column_sums(dfirst)
        sums[2:3, :] += column_sums(wide(dqkv_ref[:, :width]))
        sums[3:4, :] += column_sums(wide(dqkv_ref[:, 2 * width :]))
        sums[4:5, :] += column_sums(wide(dattn))

    def row(columns):
        return pl.BlockSpec((slots, columns), lambda i: (i, 0))

    def whole(array):
        return pl.BlockSpec(array.shape, lambda i: (0, 0), pipeline_mode=pl.Buffered(1))

    return pl.pallas_call(
        body,
        grid=(rows,),
        in_specs=[
            row(width),
            pl.BlockSpec((1, 1, slots), lambda i: (i, 0, 0)),
            row(1), whole(weights), whole(vectors), row(3 * width), row(heads), row(width),
        ],
        out_specs=(
            row(width), row(3 * width), row(width), pl.BlockSpec((8, width), lambda i: (0, 0))
        ),
        scratch_shapes=[pltpu.VMEM((slots, width), BF16)],
        out_shape=(
            jax.ShapeDtypeStruct((tokens, width), BF16),
            jax.ShapeDtypeStruct((tokens, 3 * width), BF16),
            jax.ShapeDtypeStruct((tokens, width), BF16),
            jax.ShapeDtypeStruct((8, width), F32),
        ),
        compiler_params=pltpu.CompilerParams(vmem_limit_bytes=VMEM_LIMIT),
        cost_estimate=pl.CostEstimate(
            flops=2 * tokens * width * width * 4 + 10 * rows * heads * slots * slots * HEAD_DIM,
            transcendentals=rows * heads * slots * slots,
            bytes_accessed=25 << 20,
        ),
        name="attend_back",
    )(x, across, down, weights, vectors, qkv, lse, dmid)


def attend_weights(first, dqkv, context, dattn, sums, mid_rows, down_rows, long_row, count):
    tokens, width = first.shape
    wider = long_row.shape[1]
    share, long_share = width // count, wider // count
    used = -(-(8 * share + long_share) // LANES)

    def body(
        id_ref, first_ref, dqkv_ref, ctx_ref, dattn_ref, sums_ref, mid_ref, last_ref, long_ref,
        keep_ref, send_ref, product,
    ):
        me = id_ref[0]
        turned = first_ref[...].T
        for p in range(4):
            part = slice(p * width, (p + 1) * width)
            if p < 3:
                product[...] = dot(turned, dqkv_ref[:, part])
            else:
                product[...] = dot(ctx_ref[...], dattn_ref[...], 0, 0)

            spread(
                product, share, count, me, keep_ref.at[:, :, part], send_ref.at[:, :, part]
            )

        def fold(row, shift, period):
            columns = row.shape[1]
            mine = low(jnp.where(owned(count, columns, period), row, 0.0))
            found = []
            for line in range(used):
                pick = same(LANES, columns, shift - line * LANES, period)
                found.append(dot(mine, low(pick.astype(F32)), 1, 1))
            return found

        lines = fold(long_ref[...], 8 * share, long_share)
        for v in range(8):
            source, line = ((sums_ref, v), (mid_ref, v - 5), (last_ref, 0))[(v > 4) + (v > 6)]
            row = source[line : line + 1, :]
            lines = [old + new for old, new in zip(lines, fold(row, v * share, share))]
        number = lax.broadcasted_iota(jnp.int32, (share, LANES), 0)

        def block_of(owner):
            block = jnp.zeros((share, LANES), F32)
            for line in range(used):
                block = jnp.where(number == line, lines[line][owner : owner + 1, :], block)
            return low(block)

        for couple in range(count // 2):
            slot = couple ^ (me // 2)
            even, odd = block_of(2 * couple), block_of(2 * couple + 1)
            keep_ref[slot, :, 4 * width :] = jnp.where(me % 2 == 0, even, odd)
            send_ref[slot, :, 4 * width :] = jnp.where(me % 2 == 0, odd, even)

    block = (count // 2, share, 4 * width + LANES)
    vmem = pl.BlockSpec(memory_space=pltpu.VMEM)
    return pl.pallas_call(
        body,
        in_specs=[pl.BlockSpec(memory_space=pltpu.SMEM)] + [vmem] * 8,
        out_specs=(vmem, vmem),
        out_shape=(jax.ShapeDtypeStruct(block, BF16), jax.ShapeDtypeStruct(block, BF16)),
        scratch_shapes=[pltpu.VMEM((width, width), F32)],
        compiler_params=pltpu.CompilerParams(vmem_limit_bytes=VMEM_LIMIT),
        cost_estimate=pl.CostEstimate(
            flops=2 * tokens * width * width * 4, transcendentals=0, bytes_accessed=15 << 20
        ),
        name="attend_weights",
    )(my_id(), first, dqkv, context, dattn, sums, mid_rows, down_rows, long_row)


def shards(
    layer_input, segments, cotangent, pre_gain, pre_shift, w_qkv, b_query, b_value, w_out, b_out,
    mid_gain, mid_shift, w_up, b_up, w_down, b_down,
):
    row_count, slot_count, width = layer_input.shape
    tokens = row_count * slot_count
    share, long_share = pre_gain.shape[0], b_up.shape[0]
    count = width // share
    small = [pre_gain, pre_shift, b_query, b_value, b_out, mid_gain, mid_shift, b_down, b_up]
    near = pack_near(w_qkv, w_out, small)

    near_pieces = gather_chips(near, count)
    up_pieces = gather_chips(low(w_up), count)
    down_pieces = gather_chips(low(w_down), count)
    near_all = gather_core(near_pieces, count)
    near_full = lay_out(near_all, count)

    x = layer_input.reshape(tokens, width)
    grads = cotangent.reshape(tokens, width)
    across = segments.reshape(row_count, 1, slot_count)
    down = segments.reshape(tokens, 1)
    vectors, long_bias = unpack_small(near_full, count, width, count * long_share)
    first, qkv, context, lse, middle, second = attend(x, across, down, near_full, vectors)
    up_full = lay_out(gather_core(up_pieces, count), count)
    down_full = lay_out(gather_core(down_pieces, count), count)
    result, back, down_keep, down_send, long_row, down_row = feed_forward(
        second, grads, middle, up_full, down_full, vectors, long_bias, count
    )
    dmid, up_keep, up_send, mid_rows = feed_back(
        second, back, grads, middle, up_full, vectors, count
    )
    down_total = reduce_blocks(down_keep, down_send, count)
    up_total = reduce_blocks(up_keep, up_send, count)
    dx, dqkv, dattn, sums = attend_back(x, across, down, near_full, vectors, qkv, lse, dmid)
    keep, send = attend_weights(
        first, dqkv, context, dattn, sums, mid_rows, down_row, long_row, count
    )
    total = reduce_blocks(keep, send, count)
    used = -(-(8 * share + long_share) // LANES)
    flat = total[:used, 4 * width :].reshape(-1)
    vector_grads = [flat[v * share : (v + 1) * share] for v in range(8)]
    return (
        result.reshape(layer_input.shape),
        dx.reshape(layer_input.shape),
        vector_grads[0],
        vector_grads[1],
        total[:, : 3 * width],
        vector_grads[2],
        vector_grads[3],
        total[:, 3 * width : 4 * width],
        vector_grads[4],
        vector_grads[5],
        vector_grads[6],
        up_total,
        flat[8 * share : 8 * share + long_share],
        down_total,
        vector_grads[7],
    )


def solution(mesh):
    line, table = P(AXIS), P(AXIS, None)
    cube = P(AXIS, None, None)
    return jax.shard_map(
        shards,
        mesh=mesh,
        in_specs=(
            cube, table, cube, line, line, table, line, line, table, line, line, line, table, line,
            table, line,
        ),
        out_specs=(
            cube, cube, line, line, table, line, line, table, line, line, line, table, line, table,
            line,
        ),
        check_vma=False,
    )
```

profile of v0, /device:TPU:0, one launch (start us, length us, event | category | flops | bytes accessed | tf_op | source)
XLA Modules:
  0.0 350.1 jit_solution(3548401843293049933)
XLA Ops:
  2.5 4.1 %collective-permute-start.3 = (bf16[24,3200]{1,0:T(8,128)(2,1)}, bf16[24,3200]{1,0:T(8,128)(2,1)S(1)}, u32[]{:S(2)}, u32[]{:S(2)}) collective-permute-start(bf16[24,3200]{1,0:T(8,128)(2,1)} %pack_near.1), channel_id=1, source_target_pairs={{0,16},{1,17},{2,18},{3,19},{4,20},{5,21},{6,22},{7,23},{8,24},{9,... | collective-permute-start | bytes 460808 | tf_op jit(solution)/shard_map/ppermute | solution.py:41
  15.4 15.6 %collective-permute-done.14 = bf16[24,3072]{1,0:T(8,128)(2,1)S(1)} collective-permute-done((bf16[24,3072]{1,0:T(8,128)(2,1)S(1)}, bf16[24,3072]{1,0:T(8,128)(2,1)S(1)}, u32[]{:S(2)}, u32[]{:S(2)}) %collective-permute-start.14) | collective-permute-done | bytes 147488 | tf_op jit(solution)/shard_map/ppermute | solution.py:41
  31.1 2.7 collective-permute-start.26
  33.8 9.2 %collective-permute-start.22 = (bf16[96,768]{1,0:T(8,128)(2,1)S(1)}, bf16[96,768]{1,0:T(8,128)(2,1)S(1)}, u32[]{:S(2)}, u32[]{:S(2)}) collective-permute-start(bf16[96,768]{1,0:T(8,128)(2,1)S(1)} %convert_element_type.223), channel_id=1, source_target_pairs={{0,8},{1,9},{2,10},{3,11},{4,12},{5,13},{6,14},{7,15},{8,0},{9,1},... | collective-permute-start | bytes 442376 | tf_op jit(solution)/shard_map/ppermute | solution.py:41
  45.2 2.6 collective-permute-done.22
  55.1 2.5 collective-permute-done.12
  60.0 3.9 %collective-permute-done.23 = bf16[2,96,768]{2,1,0:T(8,128)(2,1)S(1)} collective-permute-done((bf16[2,96,768]{2,1,0:T(8,128)(2,1)S(1)}, bf16[2,96,768]{2,1,0:T(8,128)(2,1)S(1)}, u32[]{:S(2)}, u32[]{:S(2)}) %collective-permute-start.23) | collective-permute-done | bytes 294944 | tf_op jit(solution)/shard_map/ppermute | solution.py:41
  65.6 14.5 %collective-permute-done.5 = bf16[2,24,3200]{2,1,0:T(8,128)(2,1)S(1)} collective-permute-done((bf16[2,24,3200]{2,1,0:T(8,128)(2,1)S(1)}, bf16[2,24,3200]{2,1,0:T(8,128)(2,1)S(1)}, u32[]{:S(2)}, u32[]{:S(2)}) %collective-permute-start.5) | collective-permute-done | bytes 307232 | tf_op jit(solution)/shard_map/ppermute | solution.py:41
  84.3 12.1 %collective-permute-done.28.refs_3_ = bf16[2,2,96,768]{3,2,1,0:T(8,128)(2,1)S(1)} collective-permute-done((bf16[2,2,96,768]{3,2,1,0:T(8,128)(2,1)S(1)}, bf16[2,2,96,768]{3,2,1,0:T(8,128)(2,1)S(1)}, u32[]{:S(2)}, u32[]{:S(2)}) %collective-permute-start.28) | collective-permute-done | bytes 589856 | tf_op jit(solution)/shard_map/ppermute | solution.py:41
  98.5 10.5 %collective-permute-done.6.refs_3_ = bf16[2,2,24,3200]{3,2,1,0:T(8,128)(2,1)S(1)} collective-permute-done((bf16[2,2,24,3200]{3,2,1,0:T(8,128)(2,1)S(1)}, bf16[2,2,24,3200]{3,2,1,0:T(8,128)(2,1)S(1)}, u32[]{:S(2)}, u32[]{:S(2)}) %collective-permute-start.6) | collective-permute-done | bytes 614432 | tf_op jit(solution)/shard_map/ppermute | solution.py:41
  109.0 2.2 collective-permute-done.2.refs_1_
  114.5 4.8 %lay_out.4 = bf16[32,24,3072]{2,1,0:T(8,128)(2,1)} custom-call(s32[1]{0:T(128)} %bitcast.id_ref, bf16[2,2,24,3072]{3,2,1,0:T(8,128)(2,1)} %copy-done.4, bf16[2,2,24,3072]{3,2,1,0:T(8,128)(2,1)} %copy-done.13, bf16[2,2,24,3072]{3,2,1,0:T(8,128)(2,1)} %copy-done.3, bf16[2,2,24,3072]{3,2,1,0:T(8,128)(2,1)} %copy-done.11, bf16[2,2,24,3072]{3,2,1,0:T(8,128)(2,1)} %copy-done.15, ...), custom_call_target="tpu_custom_call" | custom-call | tf_op jit(solution)/shard_map/lay_out/pallas_call | solution.py:90
  119.4 4.9 %lay_out.5 = bf16[32,96,768]{2,1,0:T(8,128)(2,1)} custom-call(s32[1]{0:T(128)} %bitcast.id_ref, bf16[2,2,96,768]{3,2,1,0:T(8,128)(2,1)} %copy-done.6, bf16[2,2,96,768]{3,2,1,0:T(8,128)(2,1)} %collective-permute-done.24.refs_1_, bf16[2,2,96,768]{3,2,1,0:T(8,128)(2,1)} %copy-done.5, bf16[2,2,96,768]{3,2,1,0:T(8,128)(2,1)} %copy-done.14, ...), custom_call_target="tpu_custom_call" | custom-call | tf_op jit(solution)/shard_map/lay_out/pallas_call | solution.py:90
  124.3 4.9 %lay_out.3 = bf16[32,24,3200]{2,1,0:T(8,128)(2,1)} custom-call(s32[1]{0:T(128)} %bitcast.id_ref, bf16[2,2,24,3200]{3,2,1,0:T(8,128)(2,1)} %copy-done.1, bf16[2,2,24,3200]{3,2,1,0:T(8,128)(2,1)} %copy-done.9, bf16[2,2,24,3200]{3,2,1,0:T(8,128)(2,1)} %copy-done, bf16[2,2,24,3200]{3,2,1,0:T(8,128)(2,1)} %copy-done.8, ...), custom_call_target="tpu_custom_call" | custom-call | tf_op jit(solution)/shard_map/lay_out/pallas_call | solution.py:90
  129.2 3.5 unpack_small.1
  132.7 21.0 %attend.1 = (bf16[864,768]{1,0:T(8,128)(2,1)}, bf16[864,2304]{1,0:T(8,128)(2,1)}, bf16[864,768]{1,0:T(8,128)(2,1)}, f32[864,12]{1,0:T(8,128)}, f32[864,768]{1,0:T(8,128)}, /*index=5*/bf16[864,768]{1,0:T(8,128)(2,1)}) custom-call(bf16[864,768]{1,0:T(8,128)(2,1)} %bitcast.222, s32[3,1,288]{2,1,0:T(1,128)} %reshape.127.across_ref, s32[864,1]{1,0:T(8,128)} %reshape.163.down_ref, ...), custom_call_target="tpu_custom_call" | custom-call | flops 4841275392 | bytes 31457280 | tf_op jit(solution)/shard_map/attend/pallas_call | solution.py:303
  153.7 30.0 %feed_forward.1 = (bf16[864,768]{1,0:T(8,128)(2,1)}, bf16[864,3072]{1,0:T(8,128)(2,1)}, bf16[16,96,768]{2,1,0:T(8,128)(2,1)}, bf16[16,96,768]{2,1,0:T(8,128)(2,1)}, f32[1,3072]{1,0:T(1,128)}, /*index=5*/f32[8,768]{1,0:T(8,128)}) custom-call(s32[1]{0:T(128)} %bitcast.id_ref, bf16[864,768]{1,0:T(8,128)(2,1)} %get-tuple-element.40.second_ref, ...), custom_call_target="tpu_custom_call" | custom-call | flops 16307453952 | bytes 31457280 | tf_op jit(solution)/shard_map/feed_forward/pallas_call | solution.py:367
  184.1 21.9 %feed_back.1 = (f32[864,768]{1,0:T(8,128)}, bf16[16,24,3072]{2,1,0:T(8,128)(2,1)}, bf16[16,24,3072]{2,1,0:T(8,128)(2,1)}, f32[8,768]{1,0:T(8,128)}) custom-call(s32[1]{0:T(128)} %bitcast.id_ref, bf16[864,768]{1,0:T(8,128)(2,1)} %get-tuple-element.40.second_ref, bf16[864,3072]{1,0:T(8,128)(2,1)} %get-tuple-element.46.back_ref, bf16[864,768]{1,0:T(8,128)(2,1)} %bitcast.221, ...), custom_call_target="tpu_custom_call" | custom-call | flops 8153726976 | bytes 26214400 | tf_op jit(solution)/shard_map/feed_back/pallas_call | solution.py:442
  206.1 27.4 %attend_back.1 = (bf16[864,768]{1,0:T(8,128)(2,1)}, bf16[864,2304]{1,0:T(8,128)(2,1)}, bf16[864,768]{1,0:T(8,128)(2,1)}, f32[8,768]{1,0:T(8,128)}) custom-call(bf16[864,768]{1,0:T(8,128)(2,1)} %bitcast.223, s32[3,1,288]{2,1,0:T(1,128)} %reshape.127.across_ref, s32[864,1]{1,0:T(8,128)} %reshape.163.down_ref, bf16[768,3200]{1,0:T(8,128)(2,1)} %bitcast.179, ...), custom_call_target="tpu_custom_call" | custom-call | flops 5987893248 | bytes 26214400 | tf_op jit(solution)/shard_map/attend_back/pallas_call | solution.py:538
  233.6 16.3 %attend_weights.1 = (bf16[16,24,3200]{2,1,0:T(8,128)(2,1)}, bf16[16,24,3200]{2,1,0:T(8,128)(2,1)}) custom-call(s32[1]{0:T(128)} %bitcast.id_ref, bf16[864,768]{1,0:T(8,128)(2,1)} %get-tuple-element.49.first_ref, bf16[864,2304]{1,0:T(8,128)(2,1)} %get-tuple-element.50.dqkv_ref, bf16[864,768]{1,0:T(8,128)(2,1)} %get-tuple-element.51.ctx_ref, ...), custom_call_target="tpu_custom_call" | custom-call | flops 4076863488 | bytes 15728640 | tf_op jit(solution)/shard_map/attend_weights/pallas_call | solution.py:619
  250.3 3.1 add_convert_fusion.1
  261.6 8.2 %collective-permute-done.50 = bf16[2,2,96,768]{3,2,0,1:T(8,128)(2,1)S(1)} collective-permute-done((bf16[2,2,96,768]{3,2,0,1:T(8,128)(2,1)S(1)}, bf16[2,2,96,768]{3,2,0,1:T(8,128)(2,1)S(1)}, u32[]{:S(2)}, u32[]{:S(2)}) %collective-permute-start.50) | collective-permute-done | bytes 589856 | tf_op jit(solution)/shard_map/ppermute | solution.py:41
  273.1 9.3 %collective-permute-done.42 = bf16[2,2,24,3072]{3,2,0,1:T(8,128)(2,1)S(1)} collective-permute-done((bf16[2,2,24,3072]{3,2,0,1:T(8,128)(2,1)S(1)}, bf16[2,2,24,3072]{3,2,0,1:T(8,128)(2,1)S(1)}, u32[]{:S(2)}, u32[]{:S(2)}) %collective-permute-start.42) | collective-permute-done | bytes 589856 | tf_op jit(solution)/shard_map/ppermute | solution.py:41
  285.8 9.7 %collective-permute-done.34 = bf16[2,2,24,3200]{3,2,0,1:T(8,128)(2,1)S(1)} collective-permute-done((bf16[2,2,24,3200]{3,2,0,1:T(8,128)(2,1)S(1)}, bf16[2,2,24,3200]{3,2,0,1:T(8,128)(2,1)S(1)}, u32[]{:S(2)}, u32[]{:S(2)}) %collective-permute-start.34) | collective-permute-done | bytes 614432 | tf_op jit(solution)/shard_map/ppermute | solution.py:41
  299.1 4.5 %collective-permute-done.51 = bf16[2,96,768]{2,1,0:T(8,128)(2,1)S(1)} collective-permute-done((bf16[2,96,768]{2,1,0:T(8,128)(2,1)S(1)}, bf16[2,96,768]{2,1,0:T(8,128)(2,1)S(1)}, u32[]{:S(2)}, u32[]{:S(2)}) %collective-permute-start.51) | collective-permute-done | bytes 294944 | tf_op jit(solution)/shard_map/ppermute | solution.py:41
  306.5 3.4 collective-permute-done.43
  309.9 2.2 collective-permute-start.55
  313.9 3.2 collective-permute-start.47
  318.7 2.6 collective-permute-start.56
  321.3 9.8 %collective-permute-done.47 = bf16[24,3072]{1,0:T(8,128)(2,1)S(1)} collective-permute-done((bf16[24,3072]{1,0:T(8,128)(2,1)S(1)}, bf16[24,3072]{1,0:T(8,128)(2,1)S(1)}, u32[]{:S(2)}, u32[]{:S(2)}) %collective-permute-start.47) | collective-permute-done | bytes 147488 | tf_op jit(solution)/shard_map/ppermute | solution.py:41
  331.1 4.7 %collective-permute-start.39 = (bf16[24,3200]{1,0:T(8,128)(2,1)S(1)}, bf16[24,3200]{1,0:T(8,128)(2,1)S(1)}, u32[]{:S(2)}, u32[]{:S(2)}) collective-permute-start(bf16[24,3200]{1,0:T(8,128)(2,1)S(1)} %get-tuple-element.75), channel_id=1, source_target_pairs={{0,16},{1,17},{2,18},{3,19},{4,20},{5,21},{6,22},{7,23},{8,24},{9,... | collective-permute-start | bytes 460808 | tf_op jit(solution)/shard_map/ppermute | solution.py:41
  338.8 8.5 %collective-permute-done.39 = bf16[24,3200]{1,0:T(8,128)(2,1)S(1)} collective-permute-done((bf16[24,3200]{1,0:T(8,128)(2,1)S(1)}, bf16[24,3200]{1,0:T(8,128)(2,1)S(1)}, u32[]{:S(2)}, u32[]{:S(2)}) %collective-permute-start.39) | collective-permute-done | bytes 153632 | tf_op jit(solution)/shard_map/ppermute | solution.py:41
  (201 shorter events, 64.9 us)
Async XLA Ops:
  2.5 46.7 %collective-permute-start.3 = (bf16[24,3200]{1,0:T(8,128)(2,1)}, bf16[24,3200]{1,0:T(8,128)(2,1)S(1)}, u32[]{:S(2)}, u32[]{:S(2)}) collective-permute-start(bf16[24,3200]{1,0:T(8,128)(2,1)} %pack_near.1), channel_id=1, source_target_pairs={{0,16},{1,17},{2,18},{3,19},{4,20},{5,21},{6,22},{7,23},{8,24},{9,... | collective-permute-start | bytes 460808 | tf_op jit(solution)/shard_map/ppermute | solution.py:41
  6.6 44.3 %collective-permute-start.4 = (bf16[24,3200]{1,0:T(8,128)(2,1)}, bf16[24,3200]{1,0:T(8,128)(2,1)S(1)}, u32[]{:S(2)}, u32[]{:S(2)}) collective-permute-start(bf16[24,3200]{1,0:T(8,128)(2,1)} %pack_near.1), channel_id=1, source_target_pairs={{0,24},{1,25},{2,26},{3,27},{4,28},{5,29},{6,30},{7,31},{8,16},{9,... | collective-permute-start | bytes 460808 | tf_op jit(solution)/shard_map/ppermute | solution.py:41
  8.9 22.1 %collective-permute-start.14 = (bf16[24,3072]{1,0:T(8,128)(2,1)S(1)}, bf16[24,3072]{1,0:T(8,128)(2,1)S(1)}, u32[]{:S(2)}, u32[]{:S(2)}) collective-permute-start(bf16[24,3072]{1,0:T(8,128)(2,1)S(1)} %convert_element_type.222), channel_id=1, source_target_pairs={{0,16},{1,17},{2,18},{3,19},{4,20},{5,21},{6,22},{7,23},{8,24},{9,... | collective-permute-start | bytes 442376 | tf_op jit(solution)/shard_map/ppermute | solution.py:41
  10.7 20.4 %collective-permute-start.15 = (bf16[24,3072]{1,0:T(8,128)(2,1)S(1)}, bf16[24,3072]{1,0:T(8,128)(2,1)S(1)}, u32[]{:S(2)}, u32[]{:S(2)}) collective-permute-start(bf16[24,3072]{1,0:T(8,128)(2,1)S(1)} %convert_element_type.222), channel_id=1, source_target_pairs={{0,24},{1,25},{2,26},{3,27},{4,28},{5,29},{6,30},{7,31},{8,16},{9,... | collective-permute-start | bytes 442376 | tf_op jit(solution)/shard_map/ppermute | solution.py:41
  11.6 22.2 %collective-permute-start.11 = (bf16[24,3072]{1,0:T(8,128)(2,1)S(1)}, bf16[24,3072]{1,0:T(8,128)(2,1)S(1)}, u32[]{:S(2)}, u32[]{:S(2)}) collective-permute-start(bf16[24,3072]{1,0:T(8,128)(2,1)S(1)} %convert_element_type.222), channel_id=1, source_target_pairs={{0,8},{1,9},{2,10},{3,11},{4,12},{5,13},{6,14},{7,15},{8,0},{9,1},... | collective-permute-start | bytes 442376 | tf_op jit(solution)/shard_map/ppermute | solution.py:41
  53.6 28.2 %collective-permute-start.17 = (bf16[2,2,24,3072]{3,2,1,0:T(8,128)(2,1)S(1)}, bf16[2,2,24,3072]{3,2,1,0:T(8,128)(2,1)S(1)}, u32[]{:S(2)}, u32[]{:S(2)}) collective-permute-start(bf16[2,2,24,3072]{3,2,1,0:T(8,128)(2,1)S(1)} %pad_maximum_fusion.3.refs_2_), channel_id=1, source_target_pairs={{0,2},{1,3},{2,0},{3,1},{4,6},{5,7},{6,4},{7,5},{8,10},{9,11},{10,... | collective-permute-start | bytes 1769480 | tf_op jit(solution)/shard_map/ppermute | solution.py:41
  57.6 24.2 %collective-permute-start.20 = (bf16[2,2,24,3072]{3,2,1,0:T(8,128)(2,1)S(1)}, bf16[2,2,24,3072]{3,2,1,0:T(8,128)(2,1)S(1)}, u32[]{:S(2)}, u32[]{:S(2)}) collective-permute-start(bf16[2,2,24,3072]{3,2,1,0:T(8,128)(2,1)S(1)} %pad_maximum_fusion.3.refs_2_), channel_id=1, source_target_pairs={{0,1},{1,0},{2,3},{3,2},{4,5},{5,4},{6,7},{7,6},{8,9},{9,8},{10,11... | collective-permute-start | bytes 1769480 | tf_op jit(solution)/shard_map/ppermute | solution.py:41
  57.7 25.6 %collective-permute-start.13 = (bf16[2,2,24,3072]{3,2,1,0:T(8,128)(2,1)S(1)}, bf16[2,2,24,3072]{3,2,1,0:T(8,128)(2,1)S(1)}, u32[]{:S(2)}, u32[]{:S(2)}) collective-permute-start(bf16[2,2,24,3072]{3,2,1,0:T(8,128)(2,1)S(1)} %pad_maximum_fusion.2.refs_0_), channel_id=1, source_target_pairs={{0,4},{1,5},{2,6},{3,7},{4,0},{5,1},{6,2},{7,3},{8,12},{9,13},{10,... | collective-permute-start | bytes 1769480 | tf_op jit(solution)/shard_map/ppermute | solution.py:41
  59.3 20.7 %collective-permute-start.5 = (bf16[2,24,3200]{2,1,0:T(8,128)(2,1)S(1)}, bf16[2,24,3200]{2,1,0:T(8,128)(2,1)S(1)}, u32[]{:S(2)}, u32[]{:S(2)}) collective-permute-start(bf16[2,24,3200]{2,1,0:T(8,128)(2,1)S(1)} %get-tuple-element.78), channel_id=1, source_target_pairs={{0,4},{1,5},{2,6},{3,7},{4,0},{5,1},{6,2},{7,3},{8,12},{9,13},{10,... | collective-permute-start | bytes 921608 | tf_op jit(solution)/shard_map/ppermute | solution.py:41
  63.9 16.3 %collective-permute-start.1 = (bf16[2,24,3200]{2,1,0:T(8,128)(2,1)S(1)}, bf16[2,24,3200]{2,1,0:T(8,128)(2,1)S(1)}, u32[]{:S(2)}, u32[]{:S(2)}) collective-permute-start(bf16[2,24,3200]{2,1,0:T(8,128)(2,1)S(1)} %get-tuple-element.80), channel_id=1, source_target_pairs={{0,2},{1,3},{2,0},{3,1},{4,6},{5,7},{6,4},{7,5},{8,10},{9,11},{10,... | collective-permute-start | bytes 921608 | tf_op jit(solution)/shard_map/ppermute | solution.py:41
  80.2 16.2 %collective-permute-start.28 = (bf16[2,2,96,768]{3,2,1,0:T(8,128)(2,1)S(1)}, bf16[2,2,96,768]{3,2,1,0:T(8,128)(2,1)S(1)}, u32[]{:S(2)}, u32[]{:S(2)}) collective-permute-start(bf16[2,2,96,768]{3,2,1,0:T(8,128)(2,1)S(1)} %pad_maximum_fusion.5.refs_2_), channel_id=1, source_target_pairs={{0,2},{1,3},{2,0},{3,1},{4,6},{5,7},{6,4},{7,5},{8,10},{9,11},{10,... | collective-permute-start | bytes 1769480 | tf_op jit(solution)/shard_map/ppermute | solution.py:41
  81.7 16.2 %collective-permute-start.31 = (bf16[2,2,96,768]{3,2,1,0:T(8,128)(2,1)S(1)}, bf16[2,2,96,768]{3,2,1,0:T(8,128)(2,1)S(1)}, u32[]{:S(2)}, u32[]{:S(2)}) collective-permute-start(bf16[2,2,96,768]{3,2,1,0:T(8,128)(2,1)S(1)} %pad_maximum_fusion.5.refs_2_), channel_id=1, source_target_pairs={{0,1},{1,0},{2,3},{3,2},{4,5},{5,4},{6,7},{7,6},{8,9},{9,8},{10,11... | collective-permute-start | bytes 1769480 | tf_op jit(solution)/shard_map/ppermute | solution.py:41
  81.8 16.1 %collective-permute-start.24 = (bf16[2,2,96,768]{3,2,1,0:T(8,128)(2,1)S(1)}, bf16[2,2,96,768]{3,2,1,0:T(8,128)(2,1)}, u32[]{:S(2)}, u32[]{:S(2)}) collective-permute-start(bf16[2,2,96,768]{3,2,1,0:T(8,128)(2,1)S(1)} %pad_maximum_fusion.4.refs_0_), channel_id=1, source_target_pairs={{0,4},{1,5},{2,6},{3,7},{4,0},{5,1},{6,2},{7,3},{8,12},{9,13},{10,... | collective-permute-start | bytes 1769480 | tf_op jit(solution)/shard_map/ppermute | solution.py:41
  83.7 25.3 %collective-permute-start.6 = (bf16[2,2,24,3200]{3,2,1,0:T(8,128)(2,1)S(1)}, bf16[2,2,24,3200]{3,2,1,0:T(8,128)(2,1)S(1)}, u32[]{:S(2)}, u32[]{:S(2)}) collective-permute-start(bf16[2,2,24,3200]{3,2,1,0:T(8,128)(2,1)S(1)} %pad_maximum_fusion.1.refs_2_), channel_id=1, source_target_pairs={{0,2},{1,3},{2,0},{3,1},{4,6},{5,7},{6,4},{7,5},{8,10},{9,11},{10,... | collective-permute-start | bytes 1843208 | tf_op jit(solution)/shard_map/ppermute | solution.py:41
  183.7 66.6 %collective-permute-start.49 = (bf16[16,96,768]{2,1,0:T(8,128)(2,1)}, bf16[16,96,768]{2,1,0:T(8,128)(2,1)}, u32[]{:S(2)}, u32[]{:S(2)}) collective-permute-start(bf16[16,96,768]{2,1,0:T(8,128)(2,1)} %get-tuple-element.62), channel_id=1, source_target_pairs={{0,1},{1,0},{2,3},{3,2},{4,5},{5,4},{6,7},{7,6},{8,9},{9,8},{10,11... | collective-permute-start | bytes 7077896 | tf_op jit(solution)/shard_map/ppermute | solution.py:41
  206.0 50.8 %collective-permute-start.41 = (bf16[16,24,3072]{2,1,0:T(8,128)(2,1)}, bf16[16,24,3072]{2,1,0:T(8,128)(2,1)S(1)}, u32[]{:S(2)}, u32[]{:S(2)}) collective-permute-start(bf16[16,24,3072]{2,1,0:T(8,128)(2,1)} %get-tuple-element.60), channel_id=1, source_target_pairs={{0,1},{1,0},{2,3},{3,2},{4,5},{5,4},{6,7},{7,6},{8,9},{9,8},{10,11... | collective-permute-start | bytes 7077896 | tf_op jit(solution)/shard_map/ppermute | solution.py:41
  253.5 16.3 %collective-permute-start.50 = (bf16[2,2,96,768]{3,2,0,1:T(8,128)(2,1)S(1)}, bf16[2,2,96,768]{3,2,0,1:T(8,128)(2,1)S(1)}, u32[]{:S(2)}, u32[]{:S(2)}) collective-permute-start(bf16[2,2,96,768]{3,2,0,1:T(8,128)(2,1)S(1)} %bitcast.194), channel_id=1, source_target_pairs={{0,2},{1,3},{2,0},{3,1},{4,6},{5,7},{6,4},{7,5},{8,10},{9,11},{10,... | collective-permute-start | bytes 1769480 | tf_op jit(solution)/shard_map/ppermute | solution.py:41
  255.2 16.3 %collective-permute-start.53 = (bf16[2,2,96,768]{3,2,0,1:T(8,128)(2,1)S(1)}, bf16[2,2,96,768]{3,2,0,1:T(8,128)(2,1)S(1)}, u32[]{:S(2)}, u32[]{:S(2)}) collective-permute-start(bf16[2,2,96,768]{3,2,0,1:T(8,128)(2,1)S(1)} %bitcast.192), channel_id=1, source_target_pairs={{0,4},{1,5},{2,6},{3,7},{4,0},{5,1},{6,2},{7,3},{8,12},{9,13},{10,... | collective-permute-start | bytes 1769480 | tf_op jit(solution)/shard_map/ppermute | solution.py:41
  257.8 24.6 %collective-permute-start.42 = (bf16[2,2,24,3072]{3,2,0,1:T(8,128)(2,1)S(1)}, bf16[2,2,24,3072]{3,2,0,1:T(8,128)(2,1)S(1)}, u32[]{:S(2)}, u32[]{:S(2)}) collective-permute-start(bf16[2,2,24,3072]{3,2,0,1:T(8,128)(2,1)S(1)} %bitcast.195), channel_id=1, source_target_pairs={{0,2},{1,3},{2,0},{3,1},{4,6},{5,7},{6,4},{7,5},{8,10},{9,11},{10,... | collective-permute-start | bytes 1769480 | tf_op jit(solution)/shard_map/ppermute | solution.py:41
  258.5 25.5 %collective-permute-start.45 = (bf16[2,2,24,3072]{3,2,0,1:T(8,128)(2,1)S(1)}, bf16[2,2,24,3072]{3,2,0,1:T(8,128)(2,1)S(1)}, u32[]{:S(2)}, u32[]{:S(2)}) collective-permute-start(bf16[2,2,24,3072]{3,2,0,1:T(8,128)(2,1)S(1)} %bitcast.193), channel_id=1, source_target_pairs={{0,4},{1,5},{2,6},{3,7},{4,0},{5,1},{6,2},{7,3},{8,12},{9,13},{10,... | collective-permute-start | bytes 1769480 | tf_op jit(solution)/shard_map/ppermute | solution.py:41
  260.3 35.3 %collective-permute-start.34 = (bf16[2,2,24,3200]{3,2,0,1:T(8,128)(2,1)S(1)}, bf16[2,2,24,3200]{3,2,0,1:T(8,128)(2,1)S(1)}, u32[]{:S(2)}, u32[]{:S(2)}) collective-permute-start(bf16[2,2,24,3200]{3,2,0,1:T(8,128)(2,1)S(1)} %bitcast.191), channel_id=1, source_target_pairs={{0,2},{1,3},{2,0},{3,1},{4,6},{5,7},{6,4},{7,5},{8,10},{9,11},{10,... | collective-permute-start | bytes 1843208 | tf_op jit(solution)/shard_map/ppermute | solution.py:41
  269.8 27.5 %collective-permute-start.37 = (bf16[2,2,24,3200]{3,2,0,1:T(8,128)(2,1)S(1)}, bf16[2,2,24,3200]{3,2,0,1:T(8,128)(2,1)S(1)}, u32[]{:S(2)}, u32[]{:S(2)}) collective-permute-start(bf16[2,2,24,3200]{3,2,0,1:T(8,128)(2,1)S(1)} %bitcast.190), channel_id=1, source_target_pairs={{0,4},{1,5},{2,6},{3,7},{4,0},{5,1},{6,2},{7,3},{8,12},{9,13},{10,... | collective-permute-start | bytes 1843208 | tf_op jit(solution)/shard_map/ppermute | solution.py:41
  271.5 32.1 %collective-permute-start.51 = (bf16[2,96,768]{2,1,0:T(8,128)(2,1)S(1)}, bf16[2,96,768]{2,1,0:T(8,128)(2,1)S(1)}, u32[]{:S(2)}, u32[]{:S(2)}) collective-permute-start(bf16[2,96,768]{2,1,0:T(8,128)(2,1)S(1)} %slice_bitcast_fusion.6), channel_id=1, source_target_pairs={{0,4},{1,5},{2,6},{3,7},{4,0},{5,1},{6,2},{7,3},{8,12},{9,13},{10,... | collective-permute-start | bytes 884744 | tf_op jit(solution)/shard_map/ppermute | solution.py:41
  282.4 21.8 %collective-permute-start.54 = (bf16[2,96,768]{2,1,0:T(8,128)(2,1)S(1)}, bf16[2,96,768]{2,1,0:T(8,128)(2,1)S(1)}, u32[]{:S(2)}, u32[]{:S(2)}) collective-permute-start(bf16[2,96,768]{2,1,0:T(8,128)(2,1)S(1)} %slice_bitcast_fusion.4), channel_id=1, source_target_pairs={{0,2},{1,3},{2,0},{3,1},{4,6},{5,7},{6,4},{7,5},{8,10},{9,11},{10,... | collective-permute-start | bytes 884744 | tf_op jit(solution)/shard_map/ppermute | solution.py:41
  284.1 25.8 %collective-permute-start.43 = (bf16[2,24,3072]{2,1,0:T(8,128)(2,1)S(1)}, bf16[2,24,3072]{2,1,0:T(8,128)(2,1)S(1)}, u32[]{:S(2)}, u32[]{:S(2)}) collective-permute-start(bf16[2,24,3072]{2,1,0:T(8,128)(2,1)S(1)} %slice_bitcast_fusion.10), channel_id=1, source_target_pairs={{0,4},{1,5},{2,6},{3,7},{4,0},{5,1},{6,2},{7,3},{8,12},{9,13},{10,... | collective-permute-start | bytes 884744 | tf_op jit(solution)/shard_map/ppermute | solution.py:41
  295.6 16.7 %collective-permute-start.46 = (bf16[2,24,3072]{2,1,0:T(8,128)(2,1)S(1)}, bf16[2,24,3072]{2,1,0:T(8,128)(2,1)S(1)}, u32[]{:S(2)}, u32[]{:S(2)}) collective-permute-start(bf16[2,24,3072]{2,1,0:T(8,128)(2,1)S(1)} %slice_bitcast_fusion.8), channel_id=1, source_target_pairs={{0,2},{1,3},{2,0},{3,1},{4,6},{5,7},{6,4},{7,5},{8,10},{9,11},{10,... | collective-permute-start | bytes 884744 | tf_op jit(solution)/shard_map/ppermute | solution.py:41
  297.3 20.0 %collective-permute-start.35 = (bf16[2,24,3200]{2,1,0:T(8,128)(2,1)S(1)}, bf16[2,24,3200]{2,1,0:T(8,128)(2,1)S(1)}, u32[]{:S(2)}, u32[]{:S(2)}) collective-permute-start(bf16[2,24,3200]{2,1,0:T(8,128)(2,1)S(1)} %slice_bitcast_fusion.2), channel_id=1, source_target_pairs={{0,4},{1,5},{2,6},{3,7},{4,0},{5,1},{6,2},{7,3},{8,12},{9,13},{10,... | collective-permute-start | bytes 921608 | tf_op jit(solution)/shard_map/ppermute | solution.py:41
  304.2 32.3 %collective-permute-start.52 = (bf16[96,768]{1,0:T(8,128)(2,1)S(1)}, bf16[96,768]{1,0:T(8,128)(2,1)S(1)}, u32[]{:S(2)}, u32[]{:S(2)}) collective-permute-start(bf16[96,768]{1,0:T(8,128)(2,1)S(1)} %slice_bitcast_fusion.18), channel_id=1, source_target_pairs={{0,8},{1,9},{2,10},{3,11},{4,12},{5,13},{6,14},{7,15},{8,0},{9,1},... | collective-permute-start | bytes 442376 | tf_op jit(solution)/shard_map/ppermute | solution.py:41
  309.9 28.1 %collective-permute-start.55 = (bf16[96,768]{1,0:T(8,128)(2,1)S(1)}, bf16[96,768]{1,0:T(8,128)(2,1)S(1)}, u32[]{:S(2)}, u32[]{:S(2)}) collective-permute-start(bf16[96,768]{1,0:T(8,128)(2,1)S(1)} %get-tuple-element.81), channel_id=1, source_target_pairs={{0,16},{1,17},{2,18},{3,19},{4,20},{5,21},{6,22},{7,23},{8,24},{9,... | collective-permute-start | bytes 442376 | tf_op jit(solution)/shard_map/ppermute | solution.py:41
  313.9 17.2 %collective-permute-start.47 = (bf16[24,3072]{1,0:T(8,128)(2,1)S(1)}, bf16[24,3072]{1,0:T(8,128)(2,1)S(1)}, u32[]{:S(2)}, u32[]{:S(2)}) collective-permute-start(bf16[24,3072]{1,0:T(8,128)(2,1)S(1)} %get-tuple-element.83), channel_id=1, source_target_pairs={{0,16},{1,17},{2,18},{3,19},{4,20},{5,21},{6,22},{7,23},{8,24},{9,... | collective-permute-start | bytes 442376 | tf_op jit(solution)/shard_map/ppermute | solution.py:41
  318.7 19.2 %collective-permute-start.56 = (bf16[96,768]{1,0:T(8,128)(2,1)S(1)}, bf16[96,768]{1,0:T(8,128)(2,1)S(1)}, u32[]{:S(2)}, u32[]{:S(2)}) collective-permute-start(bf16[96,768]{1,0:T(8,128)(2,1)S(1)} %get-tuple-element.82), channel_id=1, source_target_pairs={{0,24},{1,25},{2,26},{3,27},{4,28},{5,29},{6,30},{7,31},{8,16},{9,... | collective-permute-start | bytes 442376 | tf_op jit(solution)/shard_map/ppermute | solution.py:41
  331.1 16.2 %collective-permute-start.39 = (bf16[24,3200]{1,0:T(8,128)(2,1)S(1)}, bf16[24,3200]{1,0:T(8,128)(2,1)S(1)}, u32[]{:S(2)}, u32[]{:S(2)}) collective-permute-start(bf16[24,3200]{1,0:T(8,128)(2,1)S(1)} %get-tuple-element.75), channel_id=1, source_target_pairs={{0,16},{1,17},{2,18},{3,19},{4,20},{5,21},{6,22},{7,23},{8,24},{9,... | collective-permute-start | bytes 460808 | tf_op jit(solution)/shard_map/ppermute | solution.py:41
  (47 other events, 792.6 us)
where the time goes:
time: 355 us; the launch traced here: 350 us
  Pallas kernels  136 us (38%)
  waiting for transfers between devices  121 us (34%)
  starting transfers between devices  73.8 us (21%)
  other arithmetic  12 us (3%)
  local copies, waits for them, and re-layouts  5.65 us (2%)
    ppermute x57, waiting for transfers between devices, swap(): return lax.ppermute(value, AXIS, [(i, i ^ mask) for i in range(count)])  121 us
    ppermute x57, starting transfers between devices, swap(): return lax.ppermute(value, AXIS, [(i, i ^ mask) for i in range(count)])  73.8 us
    pallas_call x1, Pallas kernels, feed_forward(): pl.pallas_call(body, grid_spec=pltpu.PrefetchScalarGridSpec(num_scalar_pr...  30 us
    pallas_call x1, Pallas kernels, attend_back(): pl.pallas_call(body, grid=(rows,), in_specs=[row(width), pl.BlockSpec((1,...  27.4 us
    pallas_call x1, Pallas kernels, feed_back(): pl.pallas_call(body, grid_spec=pltpu.PrefetchScalarGridSpec(num_scalar_pr...  21.9 us
    pallas_call x1, Pallas kernels, attend(): pl.pallas_call(body, grid=(rows,), out_shape=tuple((jax.ShapeDtypeStruct(...  21 us
    pallas_call x1, Pallas kernels, attend_weights(): pl.pallas_call(body, in_specs=[pl.BlockSpec(memory_space=pltpu.SMEM)] + [...  16.3 us
    pallas_call x3, Pallas kernels, lay_out(): pl.pallas_call(body, out_shape=jax.ShapeDtypeStruct((count,) + block, pie...  14.6 us
  transfers between devices with their start and end apart: 57, of which 18 were waited for; matrix products, arithmetic and copies ran while one was open for 4% of the time, Pallas kernels for 21%

commit v1 on v0

--- a/solution.py
+++ b/solution.py
@@ -12,6 +12,7 @@
 BLOCKED = -1e9
 AXIS = "fsdp"
 FF_TILE = 384
+GROUP = 2
 VMEM_LIMIT = 60 << 20
 F32 = jnp.float32
 BF16 = jnp.bfloat16
@@ -271,11 +272,13 @@
             qkv_ref[:, part * width : (part + 1) * width] = low(product)
         bias = mask_of(across_ref[0], down_ref[...])
         masks = halves()
-        for pair in range(heads // 2):
-            lanes = slice(pair * PAIR, (pair + 1) * PAIR)
-            q = qkv_ref[:, lanes]
-            k = qkv_ref[:, width + pair * PAIR : width + (pair + 1) * PAIR]
-            v = qkv_ref[:, 2 * width + pair * PAIR : 2 * width + (pair + 1) * PAIR]
+        place = lax.broadcasted_iota(jnp.int32, (slots, heads), 1)
+
+        def couple(pair, found):
+            def lanes(part):
+                return pl.ds(pl.multiple_of(part * width + pair * PAIR, PAIR), PAIR)
+
+            q, k, v = (qkv_ref[:, lanes(part)] for part in range(3))
             context = jnp.zeros((slots, PAIR), F32)
             for side in range(2):
                 scores = dot(q * masks[side], k, 1, 1) * HEAD_DIM**-0.5 + bias
@@ -284,9 +287,18 @@
                 total = jnp.sum(powers, axis=-1, keepdims=True)
                 probs = low(powers * (1.0 / total))
                 context = context + dot(probs, v * masks[side])
-                head = 2 * pair + side
-                lse_ref[:, head : head + 1] = highest + jnp.log(total)
-            ctx_ref[:, lanes] = low(context)
+                found = jnp.where(place == 2 * pair + side, highest + jnp.log(total), found)
+            ctx_ref[:, lanes(0)] = low(context)
+            return found
+
+        def several(step, found):
+            for offset in range(GROUP):
+                found = couple(step * GROUP + offset, found)
+            return found
+
+        lse_ref[...] = lax.fori_loop(
+            0, heads // 2 // GROUP, several, jnp.zeros((slots, heads), F32)
+        )
         attention = dot(ctx_ref[...], w_ref[:, 3 * width : 4 * width]) + vec_ref[4:5, :]
         middle = value + attention
         mid_ref[...] = middle
@@ -496,27 +508,40 @@
         dctx[...] = low(dot(dattn, w_ref[:, 3 * width : 4 * width], 1, 1))
         bias = mask_of(across_ref[0], down_ref[...])
         masks = halves()
-        for pair in range(heads // 2):
-            lanes = [slice(p * width + pair * PAIR, p * width + (pair + 1) * PAIR) for p in range(3)]
-            q, k, v = (qkv_ref[:, lane] for lane in lanes)
-            dout = dctx[:, lanes[0]]
+        place = lax.broadcasted_iota(jnp.int32, (slots, heads), 1)
+
+        def couple(pair):
+            def lanes(part):
+                return pl.ds(pl.multiple_of(part * width + pair * PAIR, PAIR), PAIR)
+
+            mine = pl.ds(0, slots)
+            q, k, v = (qkv_ref[mine, lanes(part)] for part in range(3))
+            dout = dctx[:, lanes(0)]
             dq = jnp.zeros((slots, PAIR), F32)
             dk = jnp.zeros((slots, PAIR), F32)
             dv = jnp.zeros((slots, PAIR), F32)
             for side in range(2):
-                head = 2 * pair + side
+                kept = jnp.where(place == 2 * pair + side, lse_ref[...], 0.0)
+                kept = jnp.sum(kept, axis=-1, keepdims=True)
                 q_half, dout_half = q * masks[side], dout * masks[side]
                 scores = dot(q_half, k, 1, 1) * HEAD_DIM**-0.5 + bias
-                probs = jnp.exp(scores - lse_ref[:, head : head + 1])
+                probs = jnp.exp(scores - kept)
                 dprobs = dot(dout_half, v, 1, 1)
                 weighted = probs * dprobs
                 dscores = low(weighted - probs * jnp.sum(weighted, axis=-1, keepdims=True))
                 dv = dv + dot(low(probs), dout_half, 0, 0)
                 dq = dq + dot(dscores, k * masks[side])
                 dk = dk + dot(dscores, q_half, 0, 0)
-            dqkv_ref[:, lanes[0]] = low(dq * HEAD_DIM**-0.5)
-            dqkv_ref[:, lanes[1]] = low(dk * HEAD_DIM**-0.5)
-            dqkv_ref[:, lanes[2]] = low(dv)
+            dqkv_ref[:, lanes(0)] = low(dq * HEAD_DIM**-0.5)
+            dqkv_ref[:, lanes(1)] = low(dk * HEAD_DIM**-0.5)
+            dqkv_ref[:, lanes(2)] = low(dv)
+
+        def several(step, carry):
+            for offset in range(GROUP):
+                couple(step * GROUP + offset)
+            return carry
+
+        lax.fori_loop(0, heads // 2 // GROUP, several, 0)
         dfirst = jnp.zeros((slots, width), F32)
         for p in range(3):
             part = slice(p * width, (p + 1) * width)

time: 355 us -> 352 us (level); the launches traced: 350 us -> 352 us
  no operation moved by 1% of the time
where the time goes in v1:
time: 352 us
  Pallas kernels  138 us (39%)
  waiting for transfers between devices  120 us (34%)
  starting transfers between devices  73.8 us (21%)
  other arithmetic  12 us (3%)
  local copies, waits for them, and re-layouts  5.65 us (2%)
    ppermute x57, waiting for transfers between devices, swap(): return lax.ppermute(value, AXIS, [(i, i ^ mask) for i in range(count)])  120 us
    ppermute x57, starting transfers between devices, swap(): return lax.ppermute(value, AXIS, [(i, i ^ mask) for i in range(count)])  73.8 us
    pallas_call x1, Pallas kernels, feed_forward(): pl.pallas_call(body, grid_spec=pltpu.PrefetchScalarGridSpec(num_scalar_pr...  30 us
    pallas_call x1, Pallas kernels, attend_back(): pl.pallas_call(body, grid=(rows,), in_specs=[row(width), pl.BlockSpec((1,...  27.6 us
    pallas_call x1, Pallas kernels, attend(): pl.pallas_call(body, grid=(rows,), out_shape=tuple((jax.ShapeDtypeStruct(...  22.5 us
    pallas_call x1, Pallas kernels, feed_back(): pl.pallas_call(body, grid_spec=pltpu.PrefetchScalarGridSpec(num_scalar_pr...  21.7 us
    pallas_call x1, Pallas kernels, attend_weights(): pl.pallas_call(body, in_specs=[pl.BlockSpec(memory_space=pltpu.SMEM)] + [...  16.6 us
    pallas_call x3, Pallas kernels, lay_out(): pl.pallas_call(body, out_shape=jax.ShapeDtypeStruct((count,) + block, pie...  14.6 us
  transfers between devices with their start and end apart: 57, of which 18 were waited for; matrix products, arithmetic and copies ran while one was open for 4% of the time, Pallas kernels for 21%

profile of v1, /device:TPU:0, one launch (start us, length us, event | category | flops | bytes accessed | tf_op | source)
XLA Modules:
  0.0 351.7 jit_solution(17076198380551056107)
XLA Ops:
  2.5 4.1 %collective-permute-start.3 = (bf16[24,3200]{1,0:T(8,128)(2,1)}, bf16[24,3200]{1,0:T(8,128)(2,1)S(1)}, u32[]{:S(2)}, u32[]{:S(2)}) collective-permute-start(bf16[24,3200]{1,0:T(8,128)(2,1)} %pack_near.1), channel_id=1, source_target_pairs={{0,16},{1,17},{2,18},{3,19},{4,20},{5,21},{6,22},{7,23},{8,24},{9,... | collective-permute-start | bytes 460808 | tf_op jit(solution)/shard_map/ppermute | solution.py:42
  15.4 15.6 %collective-permute-done.14 = bf16[24,3072]{1,0:T(8,128)(2,1)S(1)} collective-permute-done((bf16[24,3072]{1,0:T(8,128)(2,1)S(1)}, bf16[24,3072]{1,0:T(8,128)(2,1)S(1)}, u32[]{:S(2)}, u32[]{:S(2)}) %collective-permute-start.14) | collective-permute-done | bytes 147488 | tf_op jit(solution)/shard_map/ppermute | solution.py:42
  31.1 2.7 collective-permute-start.26
  33.8 9.2 %collective-permute-start.22 = (bf16[96,768]{1,0:T(8,128)(2,1)S(1)}, bf16[96,768]{1,0:T(8,128)(2,1)S(1)}, u32[]{:S(2)}, u32[]{:S(2)}) collective-permute-start(bf16[96,768]{1,0:T(8,128)(2,1)S(1)} %convert_element_type.223), channel_id=1, source_target_pairs={{0,8},{1,9},{2,10},{3,11},{4,12},{5,13},{6,14},{7,15},{8,0},{9,1},... | collective-permute-start | bytes 442376 | tf_op jit(solution)/shard_map/ppermute | solution.py:42
  45.2 2.6 collective-permute-done.22
  55.1 2.5 collective-permute-done.12
  60.0 3.9 %collective-permute-done.23 = bf16[2,96,768]{2,1,0:T(8,128)(2,1)S(1)} collective-permute-done((bf16[2,96,768]{2,1,0:T(8,128)(2,1)S(1)}, bf16[2,96,768]{2,1,0:T(8,128)(2,1)S(1)}, u32[]{:S(2)}, u32[]{:S(2)}) %collective-permute-start.23) | collective-permute-done | bytes 294944 | tf_op jit(solution)/shard_map/ppermute | solution.py:42
  65.6 14.5 %collective-permute-done.5 = bf16[2,24,3200]{2,1,0:T(8,128)(2,1)S(1)} collective-permute-done((bf16[2,24,3200]{2,1,0:T(8,128)(2,1)S(1)}, bf16[2,24,3200]{2,1,0:T(8,128)(2,1)S(1)}, u32[]{:S(2)}, u32[]{:S(2)}) %collective-permute-start.5) | collective-permute-done | bytes 307232 | tf_op jit(solution)/shard_map/ppermute | solution.py:42
  84.3 12.1 %collective-permute-done.28.refs_3_ = bf16[2,2,96,768]{3,2,1,0:T(8,128)(2,1)S(1)} collective-permute-done((bf16[2,2,96,768]{3,2,1,0:T(8,128)(2,1)S(1)}, bf16[2,2,96,768]{3,2,1,0:T(8,128)(2,1)S(1)}, u32[]{:S(2)}, u32[]{:S(2)}) %collective-permute-start.28) | collective-permute-done | bytes 589856 | tf_op jit(solution)/shard_map/ppermute | solution.py:42
  98.5 10.5 %collective-permute-done.6.refs_3_ = bf16[2,2,24,3200]{3,2,1,0:T(8,128)(2,1)S(1)} collective-permute-done((bf16[2,2,24,3200]{3,2,1,0:T(8,128)(2,1)S(1)}, bf16[2,2,24,3200]{3,2,1,0:T(8,128)(2,1)S(1)}, u32[]{:S(2)}, u32[]{:S(2)}) %collective-permute-start.6) | collective-permute-done | bytes 614432 | tf_op jit(solution)/shard_map/ppermute | solution.py:42
  114.5 4.8 %lay_out.4 = bf16[32,24,3072]{2,1,0:T(8,128)(2,1)} custom-call(s32[1]{0:T(128)} %bitcast.id_ref, bf16[2,2,24,3072]{3,2,1,0:T(8,128)(2,1)} %copy-done.4, bf16[2,2,24,3072]{3,2,1,0:T(8,128)(2,1)} %copy-done.13, bf16[2,2,24,3072]{3,2,1,0:T(8,128)(2,1)} %copy-done.3, bf16[2,2,24,3072]{3,2,1,0:T(8,128)(2,1)} %copy-done.11, bf16[2,2,24,3072]{3,2,1,0:T(8,128)(2,1)} %copy-done.15, ...), custom_call_target="tpu_custom_call" | custom-call | tf_op jit(solution)/shard_map/lay_out/pallas_call | solution.py:91
  119.4 4.9 %lay_out.5 = bf16[32,96,768]{2,1,0:T(8,128)(2,1)} custom-call(s32[1]{0:T(128)} %bitcast.id_ref, bf16[2,2,96,768]{3,2,1,0:T(8,128)(2,1)} %copy-done.6, bf16[2,2,96,768]{3,2,1,0:T(8,128)(2,1)} %collective-permute-done.24.refs_1_, bf16[2,2,96,768]{3,2,1,0:T(8,128)(2,1)} %copy-done.5, bf16[2,2,96,768]{3,2,1,0:T(8,128)(2,1)} %copy-done.14, ...), custom_call_target="tpu_custom_call" | custom-call | tf_op jit(solution)/shard_map/lay_out/pallas_call | solution.py:91
  124.3 4.9 %lay_out.3 = bf16[32,24,3200]{2,1,0:T(8,128)(2,1)} custom-call(s32[1]{0:T(128)} %bitcast.id_ref, bf16[2,2,24,3200]{3,2,1,0:T(8,128)(2,1)} %copy-done.1, bf16[2,2,24,3200]{3,2,1,0:T(8,128)(2,1)} %copy-done.9, bf16[2,2,24,3200]{3,2,1,0:T(8,128)(2,1)} %copy-done, bf16[2,2,24,3200]{3,2,1,0:T(8,128)(2,1)} %copy-done.8, ...), custom_call_target="tpu_custom_call" | custom-call | tf_op jit(solution)/shard_map/lay_out/pallas_call | solution.py:91
  129.2 3.5 unpack_small.1
  132.7 22.5 %attend.1 = (bf16[864,768]{1,0:T(8,128)(2,1)}, bf16[864,2304]{1,0:T(8,128)(2,1)}, bf16[864,768]{1,0:T(8,128)(2,1)}, f32[864,12]{1,0:T(8,128)}, f32[864,768]{1,0:T(8,128)}, /*index=5*/bf16[864,768]{1,0:T(8,128)(2,1)}) custom-call(bf16[864,768]{1,0:T(8,128)(2,1)} %bitcast.222, s32[3,1,288]{2,1,0:T(1,128)} %reshape.127.across_ref, s32[864,1]{1,0:T(8,128)} %reshape.163.down_ref, ...), custom_call_target="tpu_custom_call" | custom-call | flops 4841275392 | bytes 31457280 | tf_op jit(solution)/shard_map/attend/pallas_call | solution.py:315
  155.2 30.0 %feed_forward.1 = (bf16[864,768]{1,0:T(8,128)(2,1)}, bf16[864,3072]{1,0:T(8,128)(2,1)}, bf16[16,96,768]{2,1,0:T(8,128)(2,1)}, bf16[16,96,768]{2,1,0:T(8,128)(2,1)}, f32[1,3072]{1,0:T(1,128)}, /*index=5*/f32[8,768]{1,0:T(8,128)}) custom-call(s32[1]{0:T(128)} %bitcast.id_ref, bf16[864,768]{1,0:T(8,128)(2,1)} %get-tuple-element.40.second_ref, ...), custom_call_target="tpu_custom_call" | custom-call | flops 16307453952 | bytes 31457280 | tf_op jit(solution)/shard_map/feed_forward/pallas_call | solution.py:379
  185.6 21.7 %feed_back.1 = (f32[864,768]{1,0:T(8,128)}, bf16[16,24,3072]{2,1,0:T(8,128)(2,1)}, bf16[16,24,3072]{2,1,0:T(8,128)(2,1)}, f32[8,768]{1,0:T(8,128)}) custom-call(s32[1]{0:T(128)} %bitcast.id_ref, bf16[864,768]{1,0:T(8,128)(2,1)} %get-tuple-element.40.second_ref, bf16[864,3072]{1,0:T(8,128)(2,1)} %get-tuple-element.46.back_ref, bf16[864,768]{1,0:T(8,128)(2,1)} %bitcast.221, ...), custom_call_target="tpu_custom_call" | custom-call | flops 8153726976 | bytes 26214400 | tf_op jit(solution)/shard_map/feed_back/pallas_call | solution.py:454
  207.5 27.6 %attend_back.1 = (bf16[864,768]{1,0:T(8,128)(2,1)}, bf16[864,2304]{1,0:T(8,128)(2,1)}, bf16[864,768]{1,0:T(8,128)(2,1)}, f32[8,768]{1,0:T(8,128)}) custom-call(bf16[864,768]{1,0:T(8,128)(2,1)} %bitcast.223, s32[3,1,288]{2,1,0:T(1,128)} %reshape.127.across_ref, s32[864,1]{1,0:T(8,128)} %reshape.163.down_ref, bf16[768,3200]{1,0:T(8,128)(2,1)} %bitcast.179, ...), custom_call_target="tpu_custom_call" | custom-call | flops 5987893248 | bytes 26214400 | tf_op jit(solution)/shard_map/attend_back/pallas_call | solution.py:563
  235.1 16.6 %attend_weights.1 = (bf16[16,24,3200]{2,1,0:T(8,128)(2,1)}, bf16[16,24,3200]{2,1,0:T(8,128)(2,1)}) custom-call(s32[1]{0:T(128)} %bitcast.id_ref, bf16[864,768]{1,0:T(8,128)(2,1)} %get-tuple-element.49.first_ref, bf16[864,2304]{1,0:T(8,128)(2,1)} %get-tuple-element.50.dqkv_ref, bf16[864,768]{1,0:T(8,128)(2,1)} %get-tuple-element.51.ctx_ref, ...), custom_call_target="tpu_custom_call" | custom-call | flops 4076863488 | bytes 15728640 | tf_op jit(solution)/shard_map/attend_weights/pallas_call | solution.py:644
  252.0 3.1 add_convert_fusion.1
  263.3 8.2 %collective-permute-done.50 = bf16[2,2,96,768]{3,2,0,1:T(8,128)(2,1)S(1)} collective-permute-done((bf16[2,2,96,768]{3,2,0,1:T(8,128)(2,1)S(1)}, bf16[2,2,96,768]{3,2,0,1:T(8,128)(2,1)S(1)}, u32[]{:S(2)}, u32[]{:S(2)}) %collective-permute-start.50) | collective-permute-done | bytes 589856 | tf_op jit(solution)/shard_map/ppermute | solution.py:42
  274.9 9.2 %collective-permute-done.42 = bf16[2,2,24,3072]{3,2,0,1:T(8,128)(2,1)S(1)} collective-permute-done((bf16[2,2,24,3072]{3,2,0,1:T(8,128)(2,1)S(1)}, bf16[2,2,24,3072]{3,2,0,1:T(8,128)(2,1)S(1)}, u32[]{:S(2)}, u32[]{:S(2)}) %collective-permute-start.42) | collective-permute-done | bytes 589856 | tf_op jit(solution)/shard_map/ppermute | solution.py:42
  287.6 9.7 %collective-permute-done.34 = bf16[2,2,24,3200]{3,2,0,1:T(8,128)(2,1)S(1)} collective-permute-done((bf16[2,2,24,3200]{3,2,0,1:T(8,128)(2,1)S(1)}, bf16[2,2,24,3200]{3,2,0,1:T(8,128)(2,1)S(1)}, u32[]{:S(2)}, u32[]{:S(2)}) %collective-permute-start.34) | collective-permute-done | bytes 614432 | tf_op jit(solution)/shard_map/ppermute | solution.py:42
  300.8 4.5 %collective-permute-done.51 = bf16[2,96,768]{2,1,0:T(8,128)(2,1)S(1)} collective-permute-done((bf16[2,96,768]{2,1,0:T(8,128)(2,1)S(1)}, bf16[2,96,768]{2,1,0:T(8,128)(2,1)S(1)}, u32[]{:S(2)}, u32[]{:S(2)}) %collective-permute-start.51) | collective-permute-done | bytes 294944 | tf_op jit(solution)/shard_map/ppermute | solution.py:42
  306.0 2.2 collective-permute-start.52
  308.3 3.3 collective-permute-done.43
  311.6 2.2 collective-permute-start.55
  315.7 3.2 collective-permute-start.47
  320.5 2.6 collective-permute-start.56
  323.1 9.8 %collective-permute-done.47 = bf16[24,3072]{1,0:T(8,128)(2,1)S(1)} collective-permute-done((bf16[24,3072]{1,0:T(8,128)(2,1)S(1)}, bf16[24,3072]{1,0:T(8,128)(2,1)S(1)}, u32[]{:S(2)}, u32[]{:S(2)}) %collective-permute-start.47) | collective-permute-done | bytes 147488 | tf_op jit(solution)/shard_map/ppermute | solution.py:42
  332.9 4.7 %collective-permute-start.39 = (bf16[24,3200]{1,0:T(8,128)(2,1)S(1)}, bf16[24,3200]{1,0:T(8,128)(2,1)S(1)}, u32[]{:S(2)}, u32[]{:S(2)}) collective-permute-start(bf16[24,3200]{1,0:T(8,128)(2,1)S(1)} %get-tuple-element.75), channel_id=1, source_target_pairs={{0,16},{1,17},{2,18},{3,19},{4,20},{5,21},{6,22},{7,23},{8,24},{9,... | collective-permute-start | bytes 460808 | tf_op jit(solution)/shard_map/ppermute | solution.py:42
  340.5 8.5 %collective-permute-done.39 = bf16[24,3200]{1,0:T(8,128)(2,1)S(1)} collective-permute-done((bf16[24,3200]{1,0:T(8,128)(2,1)S(1)}, bf16[24,3200]{1,0:T(8,128)(2,1)S(1)}, u32[]{:S(2)}, u32[]{:S(2)}) %collective-permute-start.39) | collective-permute-done | bytes 153632 | tf_op jit(solution)/shard_map/ppermute | solution.py:42
  (201 shorter events, 64.9 us)
Async XLA Ops:
  2.5 46.7 %collective-permute-start.3 = (bf16[24,3200]{1,0:T(8,128)(2,1)}, bf16[24,3200]{1,0:T(8,128)(2,1)S(1)}, u32[]{:S(2)}, u32[]{:S(2)}) collective-permute-start(bf16[24,3200]{1,0:T(8,128)(2,1)} %pack_near.1), channel_id=1, source_target_pairs={{0,16},{1,17},{2,18},{3,19},{4,20},{5,21},{6,22},{7,23},{8,24},{9,... | collective-permute-start | bytes 460808 | tf_op jit(solution)/shard_map/ppermute | solution.py:42
  6.6 44.3 %collective-permute-start.4 = (bf16[24,3200]{1,0:T(8,128)(2,1)}, bf16[24,3200]{1,0:T(8,128)(2,1)S(1)}, u32[]{:S(2)}, u32[]{:S(2)}) collective-permute-start(bf16[24,3200]{1,0:T(8,128)(2,1)} %pack_near.1), channel_id=1, source_target_pairs={{0,24},{1,25},{2,26},{3,27},{4,28},{5,29},{6,30},{7,31},{8,16},{9,... | collective-permute-start | bytes 460808 | tf_op jit(solution)/shard_map/ppermute | solution.py:42
  8.9 22.1 %collective-permute-start.14 = (bf16[24,3072]{1,0:T(8,128)(2,1)S(1)}, bf16[24,3072]{1,0:T(8,128)(2,1)S(1)}, u32[]{:S(2)}, u32[]{:S(2)}) collective-permute-start(bf16[24,3072]{1,0:T(8,128)(2,1)S(1)} %convert_element_type.222), channel_id=1, source_target_pairs={{0,16},{1,17},{2,18},{3,19},{4,20},{5,21},{6,22},{7,23},{8,24},{9,... | collective-permute-start | bytes 442376 | tf_op jit(solution)/shard_map/ppermute | solution.py:42
  10.7 20.4 %collective-permute-start.15 = (bf16[24,3072]{1,0:T(8,128)(2,1)S(1)}, bf16[24,3072]{1,0:T(8,128)(2,1)S(1)}, u32[]{:S(2)}, u32[]{:S(2)}) collective-permute-start(bf16[24,3072]{1,0:T(8,128)(2,1)S(1)} %convert_element_type.222), channel_id=1, source_target_pairs={{0,24},{1,25},{2,26},{3,27},{4,28},{5,29},{6,30},{7,31},{8,16},{9,... | collective-permute-start | bytes 442376 | tf_op jit(solution)/shard_map/ppermute | solution.py:42
  11.6 22.2 %collective-permute-start.11 = (bf16[24,3072]{1,0:T(8,128)(2,1)S(1)}, bf16[24,3072]{1,0:T(8,128)(2,1)S(1)}, u32[]{:S(2)}, u32[]{:S(2)}) collective-permute-start(bf16[24,3072]{1,0:T(8,128)(2,1)S(1)} %convert_element_type.222), channel_id=1, source_target_pairs={{0,8},{1,9},{2,10},{3,11},{4,12},{5,13},{6,14},{7,15},{8,0},{9,1},... | collective-permute-start | bytes 442376 | tf_op jit(solution)/shard_map/ppermute | solution.py:42
  53.6 28.2 %collective-permute-start.17 = (bf16[2,2,24,3072]{3,2,1,0:T(8,128)(2,1)S(1)}, bf16[2,2,24,3072]{3,2,1,0:T(8,128)(2,1)S(1)}, u32[]{:S(2)}, u32[]{:S(2)}) collective-permute-start(bf16[2,2,24,3072]{3,2,1,0:T(8,128)(2,1)S(1)} %pad_maximum_fusion.3.refs_2_), channel_id=1, source_target_pairs={{0,2},{1,3},{2,0},{3,1},{4,6},{5,7},{6,4},{7,5},{8,10},{9,11},{10,... | collective-permute-start | bytes 1769480 | tf_op jit(solution)/shard_map/ppermute | solution.py:42
  57.6 24.2 %collective-permute-start.20 = (bf16[2,2,24,3072]{3,2,1,0:T(8,128)(2,1)S(1)}, bf16[2,2,24,3072]{3,2,1,0:T(8,128)(2,1)S(1)}, u32[]{:S(2)}, u32[]{:S(2)}) collective-permute-start(bf16[2,2,24,3072]{3,2,1,0:T(8,128)(2,1)S(1)} %pad_maximum_fusion.3.refs_2_), channel_id=1, source_target_pairs={{0,1},{1,0},{2,3},{3,2},{4,5},{5,4},{6,7},{7,6},{8,9},{9,8},{10,11... | collective-permute-start | bytes 1769480 | tf_op jit(solution)/shard_map/ppermute | solution.py:42
  57.7 25.6 %collective-permute-start.13 = (bf16[2,2,24,3072]{3,2,1,0:T(8,128)(2,1)S(1)}, bf16[2,2,24,3072]{3,2,1,0:T(8,128)(2,1)S(1)}, u32[]{:S(2)}, u32[]{:S(2)}) collective-permute-start(bf16[2,2,24,3072]{3,2,1,0:T(8,128)(2,1)S(1)} %pad_maximum_fusion.2.refs_0_), channel_id=1, source_target_pairs={{0,4},{1,5},{2,6},{3,7},{4,0},{5,1},{6,2},{7,3},{8,12},{9,13},{10,... | collective-permute-start | bytes 1769480 | tf_op jit(solution)/shard_map/ppermute | solution.py:42
  59.3 20.7 %collective-permute-start.5 = (bf16[2,24,3200]{2,1,0:T(8,128)(2,1)S(1)}, bf16[2,24,3200]{2,1,0:T(8,128)(2,1)S(1)}, u32[]{:S(2)}, u32[]{:S(2)}) collective-permute-start(bf16[2,24,3200]{2,1,0:T(8,128)(2,1)S(1)} %get-tuple-element.78), channel_id=1, source_target_pairs={{0,4},{1,5},{2,6},{3,7},{4,0},{5,1},{6,2},{7,3},{8,12},{9,13},{10,... | collective-permute-start | bytes 921608 | tf_op jit(solution)/shard_map/ppermute | solution.py:42
  63.9 16.3 %collective-permute-start.1 = (bf16[2,24,3200]{2,1,0:T(8,128)(2,1)S(1)}, bf16[2,24,3200]{2,1,0:T(8,128)(2,1)S(1)}, u32[]{:S(2)}, u32[]{:S(2)}) collective-permute-start(bf16[2,24,3200]{2,1,0:T(8,128)(2,1)S(1)} %get-tuple-element.80), channel_id=1, source_target_pairs={{0,2},{1,3},{2,0},{3,1},{4,6},{5,7},{6,4},{7,5},{8,10},{9,11},{10,... | collective-permute-start | bytes 921608 | tf_op jit(solution)/shard_map/ppermute | solution.py:42
  80.2 16.2 %collective-permute-start.28 = (bf16[2,2,96,768]{3,2,1,0:T(8,128)(2,1)S(1)}, bf16[2,2,96,768]{3,2,1,0:T(8,128)(2,1)S(1)}, u32[]{:S(2)}, u32[]{:S(2)}) collective-permute-start(bf16[2,2,96,768]{3,2,1,0:T(8,128)(2,1)S(1)} %pad_maximum_fusion.5.refs_2_), channel_id=1, source_target_pairs={{0,2},{1,3},{2,0},{3,1},{4,6},{5,7},{6,4},{7,5},{8,10},{9,11},{10,... | collective-permute-start | bytes 1769480 | tf_op jit(solution)/shard_map/ppermute | solution.py:42
  81.7 16.2 %collective-permute-start.31 = (bf16[2,2,96,768]{3,2,1,0:T(8,128)(2,1)S(1)}, bf16[2,2,96,768]{3,2,1,0:T(8,128)(2,1)S(1)}, u32[]{:S(2)}, u32[]{:S(2)}) collective-permute-start(bf16[2,2,96,768]{3,2,1,0:T(8,128)(2,1)S(1)} %pad_maximum_fusion.5.refs_2_), channel_id=1, source_target_pairs={{0,1},{1,0},{2,3},{3,2},{4,5},{5,4},{6,7},{7,6},{8,9},{9,8},{10,11... | collective-permute-start | bytes 1769480 | tf_op jit(solution)/shard_map/ppermute | solution.py:42
  81.8 16.1 %collective-permute-start.24 = (bf16[2,2,96,768]{3,2,1,0:T(8,128)(2,1)S(1)}, bf16[2,2,96,768]{3,2,1,0:T(8,128)(2,1)}, u32[]{:S(2)}, u32[]{:S(2)}) collective-permute-start(bf16[2,2,96,768]{3,2,1,0:T(8,128)(2,1)S(1)} %pad_maximum_fusion.4.refs_0_), channel_id=1, source_target_pairs={{0,4},{1,5},{2,6},{3,7},{4,0},{5,1},{6,2},{7,3},{8,12},{9,13},{10,... | collective-permute-start | bytes 1769480 | tf_op jit(solution)/shard_map/ppermute | solution.py:42
  83.7 25.3 %collective-permute-start.6 = (bf16[2,2,24,3200]{3,2,1,0:T(8,128)(2,1)S(1)}, bf16[2,2,24,3200]{3,2,1,0:T(8,128)(2,1)S(1)}, u32[]{:S(2)}, u32[]{:S(2)}) collective-permute-start(bf16[2,2,24,3200]{3,2,1,0:T(8,128)(2,1)S(1)} %pad_maximum_fusion.1.refs_2_), channel_id=1, source_target_pairs={{0,2},{1,3},{2,0},{3,1},{4,6},{5,7},{6,4},{7,5},{8,10},{9,11},{10,... | collective-permute-start | bytes 1843208 | tf_op jit(solution)/shard_map/ppermute | solution.py:42
  185.2 66.9 %collective-permute-start.49 = (bf16[16,96,768]{2,1,0:T(8,128)(2,1)}, bf16[16,96,768]{2,1,0:T(8,128)(2,1)}, u32[]{:S(2)}, u32[]{:S(2)}) collective-permute-start(bf16[16,96,768]{2,1,0:T(8,128)(2,1)} %get-tuple-element.62), channel_id=1, source_target_pairs={{0,1},{1,0},{2,3},{3,2},{4,5},{5,4},{6,7},{7,6},{8,9},{9,8},{10,11... | collective-permute-start | bytes 7077896 | tf_op jit(solution)/shard_map/ppermute | solution.py:42
  207.3 51.2 %collective-permute-start.41 = (bf16[16,24,3072]{2,1,0:T(8,128)(2,1)}, bf16[16,24,3072]{2,1,0:T(8,128)(2,1)S(1)}, u32[]{:S(2)}, u32[]{:S(2)}) collective-permute-start(bf16[16,24,3072]{2,1,0:T(8,128)(2,1)} %get-tuple-element.60), channel_id=1, source_target_pairs={{0,1},{1,0},{2,3},{3,2},{4,5},{5,4},{6,7},{7,6},{8,9},{9,8},{10,11... | collective-permute-start | bytes 7077896 | tf_op jit(solution)/shard_map/ppermute | solution.py:42
  255.2 16.3 %collective-permute-start.50 = (bf16[2,2,96,768]{3,2,0,1:T(8,128)(2,1)S(1)}, bf16[2,2,96,768]{3,2,0,1:T(8,128)(2,1)S(1)}, u32[]{:S(2)}, u32[]{:S(2)}) collective-permute-start(bf16[2,2,96,768]{3,2,0,1:T(8,128)(2,1)S(1)} %bitcast.194), channel_id=1, source_target_pairs={{0,2},{1,3},{2,0},{3,1},{4,6},{5,7},{6,4},{7,5},{8,10},{9,11},{10,... | collective-permute-start | bytes 1769480 | tf_op jit(solution)/shard_map/ppermute | solution.py:42
  256.9 16.3 %collective-permute-start.53 = (bf16[2,2,96,768]{3,2,0,1:T(8,128)(2,1)S(1)}, bf16[2,2,96,768]{3,2,0,1:T(8,128)(2,1)S(1)}, u32[]{:S(2)}, u32[]{:S(2)}) collective-permute-start(bf16[2,2,96,768]{3,2,0,1:T(8,128)(2,1)S(1)} %bitcast.192), channel_id=1, source_target_pairs={{0,4},{1,5},{2,6},{3,7},{4,0},{5,1},{6,2},{7,3},{8,12},{9,13},{10,... | collective-permute-start | bytes 1769480 | tf_op jit(solution)/shard_map/ppermute | solution.py:42
  259.6 24.6 %collective-permute-start.42 = (bf16[2,2,24,3072]{3,2,0,1:T(8,128)(2,1)S(1)}, bf16[2,2,24,3072]{3,2,0,1:T(8,128)(2,1)S(1)}, u32[]{:S(2)}, u32[]{:S(2)}) collective-permute-start(bf16[2,2,24,3072]{3,2,0,1:T(8,128)(2,1)S(1)} %bitcast.195), channel_id=1, source_target_pairs={{0,2},{1,3},{2,0},{3,1},{4,6},{5,7},{6,4},{7,5},{8,10},{9,11},{10,... | collective-permute-start | bytes 1769480 | tf_op jit(solution)/shard_map/ppermute | solution.py:42
  260.3 25.5 %collective-permute-start.45 = (bf16[2,2,24,3072]{3,2,0,1:T(8,128)(2,1)S(1)}, bf16[2,2,24,3072]{3,2,0,1:T(8,128)(2,1)S(1)}, u32[]{:S(2)}, u32[]{:S(2)}) collective-permute-start(bf16[2,2,24,3072]{3,2,0,1:T(8,128)(2,1)S(1)} %bitcast.193), channel_id=1, source_target_pairs={{0,4},{1,5},{2,6},{3,7},{4,0},{5,1},{6,2},{7,3},{8,12},{9,13},{10,... | collective-permute-start | bytes 1769480 | tf_op jit(solution)/shard_map/ppermute | solution.py:42
  262.1 35.3 %collective-permute-start.34 = (bf16[2,2,24,3200]{3,2,0,1:T(8,128)(2,1)S(1)}, bf16[2,2,24,3200]{3,2,0,1:T(8,128)(2,1)S(1)}, u32[]{:S(2)}, u32[]{:S(2)}) collective-permute-start(bf16[2,2,24,3200]{3,2,0,1:T(8,128)(2,1)S(1)} %bitcast.191), channel_id=1, source_target_pairs={{0,2},{1,3},{2,0},{3,1},{4,6},{5,7},{6,4},{7,5},{8,10},{9,11},{10,... | collective-permute-start | bytes 1843208 | tf_op jit(solution)/shard_map/ppermute | solution.py:42
  271.5 27.5 %collective-permute-start.37 = (bf16[2,2,24,3200]{3,2,0,1:T(8,128)(2,1)S(1)}, bf16[2,2,24,3200]{3,2,0,1:T(8,128)(2,1)S(1)}, u32[]{:S(2)}, u32[]{:S(2)}) collective-permute-start(bf16[2,2,24,3200]{3,2,0,1:T(8,128)(2,1)S(1)} %bitcast.190), channel_id=1, source_target_pairs={{0,4},{1,5},{2,6},{3,7},{4,0},{5,1},{6,2},{7,3},{8,12},{9,13},{10,... | collective-permute-start | bytes 1843208 | tf_op jit(solution)/shard_map/ppermute | solution.py:42
  273.2 32.1 %collective-permute-start.51 = (bf16[2,96,768]{2,1,0:T(8,128)(2,1)S(1)}, bf16[2,96,768]{2,1,0:T(8,128)(2,1)S(1)}, u32[]{:S(2)}, u32[]{:S(2)}) collective-permute-start(bf16[2,96,768]{2,1,0:T(8,128)(2,1)S(1)} %slice_bitcast_fusion.6), channel_id=1, source_target_pairs={{0,4},{1,5},{2,6},{3,7},{4,0},{5,1},{6,2},{7,3},{8,12},{9,13},{10,... | collective-permute-start | bytes 884744 | tf_op jit(solution)/shard_map/ppermute | solution.py:42
  284.2 21.8 %collective-permute-start.54 = (bf16[2,96,768]{2,1,0:T(8,128)(2,1)S(1)}, bf16[2,96,768]{2,1,0:T(8,128)(2,1)S(1)}, u32[]{:S(2)}, u32[]{:S(2)}) collective-permute-start(bf16[2,96,768]{2,1,0:T(8,128)(2,1)S(1)} %slice_bitcast_fusion.4), channel_id=1, source_target_pairs={{0,2},{1,3},{2,0},{3,1},{4,6},{5,7},{6,4},{7,5},{8,10},{9,11},{10,... | collective-permute-start | bytes 884744 | tf_op jit(solution)/shard_map/ppermute | solution.py:42
  285.8 25.8 %collective-permute-start.43 = (bf16[2,24,3072]{2,1,0:T(8,128)(2,1)S(1)}, bf16[2,24,3072]{2,1,0:T(8,128)(2,1)S(1)}, u32[]{:S(2)}, u32[]{:S(2)}) collective-permute-start(bf16[2,24,3072]{2,1,0:T(8,128)(2,1)S(1)} %slice_bitcast_fusion.10), channel_id=1, source_target_pairs={{0,4},{1,5},{2,6},{3,7},{4,0},{5,1},{6,2},{7,3},{8,12},{9,13},{10,... | collective-permute-start | bytes 884744 | tf_op jit(solution)/shard_map/ppermute | solution.py:42
  297.3 16.7 %collective-permute-start.46 = (bf16[2,24,3072]{2,1,0:T(8,128)(2,1)S(1)}, bf16[2,24,3072]{2,1,0:T(8,128)(2,1)S(1)}, u32[]{:S(2)}, u32[]{:S(2)}) collective-permute-start(bf16[2,24,3072]{2,1,0:T(8,128)(2,1)S(1)} %slice_bitcast_fusion.8), channel_id=1, source_target_pairs={{0,2},{1,3},{2,0},{3,1},{4,6},{5,7},{6,4},{7,5},{8,10},{9,11},{10,... | collective-permute-start | bytes 884744 | tf_op jit(solution)/shard_map/ppermute | solution.py:42
  299.0 20.0 %collective-permute-start.35 = (bf16[2,24,3200]{2,1,0:T(8,128)(2,1)S(1)}, bf16[2,24,3200]{2,1,0:T(8,128)(2,1)S(1)}, u32[]{:S(2)}, u32[]{:S(2)}) collective-permute-start(bf16[2,24,3200]{2,1,0:T(8,128)(2,1)S(1)} %slice_bitcast_fusion.2), channel_id=1, source_target_pairs={{0,4},{1,5},{2,6},{3,7},{4,0},{5,1},{6,2},{7,3},{8,12},{9,13},{10,... | collective-permute-start | bytes 921608 | tf_op jit(solution)/shard_map/ppermute | solution.py:42
  306.0 32.4 %collective-permute-start.52 = (bf16[96,768]{1,0:T(8,128)(2,1)S(1)}, bf16[96,768]{1,0:T(8,128)(2,1)S(1)}, u32[]{:S(2)}, u32[]{:S(2)}) collective-permute-start(bf16[96,768]{1,0:T(8,128)(2,1)S(1)} %slice_bitcast_fusion.18), channel_id=1, source_target_pairs={{0,8},{1,9},{2,10},{3,11},{4,12},{5,13},{6,14},{7,15},{8,0},{9,1},... | collective-permute-start | bytes 442376 | tf_op jit(solution)/shard_map/ppermute | solution.py:42
  311.6 28.1 %collective-permute-start.55 = (bf16[96,768]{1,0:T(8,128)(2,1)S(1)}, bf16[96,768]{1,0:T(8,128)(2,1)S(1)}, u32[]{:S(2)}, u32[]{:S(2)}) collective-permute-start(bf16[96,768]{1,0:T(8,128)(2,1)S(1)} %get-tuple-element.81), channel_id=1, source_target_pairs={{0,16},{1,17},{2,18},{3,19},{4,20},{5,21},{6,22},{7,23},{8,24},{9,... | collective-permute-start | bytes 442376 | tf_op jit(solution)/shard_map/ppermute | solution.py:42
  315.7 17.2 %collective-permute-start.47 = (bf16[24,3072]{1,0:T(8,128)(2,1)S(1)}, bf16[24,3072]{1,0:T(8,128)(2,1)S(1)}, u32[]{:S(2)}, u32[]{:S(2)}) collective-permute-start(bf16[24,3072]{1,0:T(8,128)(2,1)S(1)} %get-tuple-element.83), channel_id=1, source_target_pairs={{0,16},{1,17},{2,18},{3,19},{4,20},{5,21},{6,22},{7,23},{8,24},{9,... | collective-permute-start | bytes 442376 | tf_op jit(solution)/shard_map/ppermute | solution.py:42
  320.5 19.2 %collective-permute-start.56 = (bf16[96,768]{1,0:T(8,128)(2,1)S(1)}, bf16[96,768]{1,0:T(8,128)(2,1)S(1)}, u32[]{:S(2)}, u32[]{:S(2)}) collective-permute-start(bf16[96,768]{1,0:T(8,128)(2,1)S(1)} %get-tuple-element.82), channel_id=1, source_target_pairs={{0,24},{1,25},{2,26},{3,27},{4,28},{5,29},{6,30},{7,31},{8,16},{9,... | collective-permute-start | bytes 442376 | tf_op jit(solution)/shard_map/ppermute | solution.py:42
  332.9 16.2 %collective-permute-start.39 = (bf16[24,3200]{1,0:T(8,128)(2,1)S(1)}, bf16[24,3200]{1,0:T(8,128)(2,1)S(1)}, u32[]{:S(2)}, u32[]{:S(2)}) collective-permute-start(bf16[24,3200]{1,0:T(8,128)(2,1)S(1)} %get-tuple-element.75), channel_id=1, source_target_pairs={{0,16},{1,17},{2,18},{3,19},{4,20},{5,21},{6,22},{7,23},{8,24},{9,... | collective-permute-start | bytes 460808 | tf_op jit(solution)/shard_map/ppermute | solution.py:42
  (47 other events, 792.6 us)

commit v2 on v1

--- a/solution.py
+++ b/solution.py
@@ -11,7 +11,7 @@
 EPSILON = 1e-06
 BLOCKED = -1e9
 AXIS = "fsdp"
-FF_TILE = 384
+FF_TILE = 768
 GROUP = 2
 VMEM_LIMIT = 60 << 20
 F32 = jnp.float32
@@ -111,8 +111,8 @@
 def reduce_blocks(keep, send, count):
     x, y, z = axes_of(count)
     shape = (z[0], y[0], x[0]) + keep.shape[1:]
-    both = wide(keep) + wide(swap(send, 1, count))
-    both = low(both).reshape(shape)
+    other = swap(send, 1, count)
+    both = low(wide(keep) + wide(other)).reshape(shape)
     half = z[0] // 2
     left = [both[:half, :, d] for d in range(x[0])]
     left = low(reduce_axis(left, x, count))
@@ -244,7 +244,7 @@
                 out[slot] = low(product[pl.ds(start, rows), :])
             return carry
 
-        lax.fori_loop(0, count // 2, place, 0)
+        lax.fori_loop(0, count // 2, place, 0, unroll=min(4, count // 2))
         return
     for couple in range(count // 2):
         slot = couple ^ (me // 2)

time: 352 us -> 344 us (0.977)
  Pallas kernels: 138 us -> 130 us
    pallas_call x1, Pallas kernels: 30 us -> 26 us  [feed_forward(): pl.pallas_call(body, grid_spec=pltpu.PrefetchScalarGridSpec(num_scalar_pr...]
where the time goes in v2:
time: 344 us
  Pallas kernels  130 us (38%)
  waiting for transfers between devices  121 us (35%)
  starting transfers between devices  73.8 us (21%)
  other arithmetic  12 us (3%)
  local copies, waits for them, and re-layouts  5.65 us (2%)
    ppermute x57, waiting for transfers between devices, swap(): return lax.ppermute(value, AXIS, [(i, i ^ mask) for i in range(count)])  121 us
    ppermute x57, starting transfers between devices, swap(): return lax.ppermute(value, AXIS, [(i, i ^ mask) for i in range(count)])  73.8 us
    pallas_call x1, Pallas kernels, attend_back(): pl.pallas_call(body, grid=(rows,), in_specs=[row(width), pl.BlockSpec((1,...  27.4 us
    pallas_call x1, Pallas kernels, feed_forward(): pl.pallas_call(body, grid_spec=pltpu.PrefetchScalarGridSpec(num_scalar_pr...  26 us
    pallas_call x1, Pallas kernels, attend(): pl.pallas_call(body, grid=(rows,), out_shape=tuple((jax.ShapeDtypeStruct(...  22.5 us
    pallas_call x1, Pallas kernels, feed_back(): pl.pallas_call(body, grid_spec=pltpu.PrefetchScalarGridSpec(num_scalar_pr...  18.3 us
    pallas_call x1, Pallas kernels, attend_weights(): pl.pallas_call(body, in_specs=[pl.BlockSpec(memory_space=pltpu.SMEM)] + [...  16.3 us
    pallas_call x3, Pallas kernels, lay_out(): pl.pallas_call(body, out_shape=jax.ShapeDtypeStruct((count,) + block, pie...  14.6 us
  transfers between devices with their start and end apart: 57, of which 18 were waited for; matrix products, arithmetic and copies ran while one was open for 4% of the time, Pallas kernels for 21%

profile of v2, /device:TPU:0, one launch (start us, length us, event | category | flops | bytes accessed | tf_op | source)
XLA Modules:
  0.0 344.1 jit_solution(10753058675186886574)
XLA Ops:
  2.5 4.1 %collective-permute-start.3 = (bf16[24,3200]{1,0:T(8,128)(2,1)}, bf16[24,3200]{1,0:T(8,128)(2,1)S(1)}, u32[]{:S(2)}, u32[]{:S(2)}) collective-permute-start(bf16[24,3200]{1,0:T(8,128)(2,1)} %pack_near.1), channel_id=1, source_target_pairs={{0,16},{1,17},{2,18},{3,19},{4,20},{5,21},{6,22},{7,23},{8,24},{9,... | collective-permute-start | bytes 460808 | tf_op jit(solution)/shard_map/ppermute | solution.py:42
  15.4 15.6 %collective-permute-done.14 = bf16[24,3072]{1,0:T(8,128)(2,1)S(1)} collective-permute-done((bf16[24,3072]{1,0:T(8,128)(2,1)S(1)}, bf16[24,3072]{1,0:T(8,128)(2,1)S(1)}, u32[]{:S(2)}, u32[]{:S(2)}) %collective-permute-start.14) | collective-permute-done | bytes 147488 | tf_op jit(solution)/shard_map/ppermute | solution.py:42
  31.1 2.7 collective-permute-start.26
  33.8 9.2 %collective-permute-start.22 = (bf16[96,768]{1,0:T(8,128)(2,1)S(1)}, bf16[96,768]{1,0:T(8,128)(2,1)S(1)}, u32[]{:S(2)}, u32[]{:S(2)}) collective-permute-start(bf16[96,768]{1,0:T(8,128)(2,1)S(1)} %convert_element_type.223), channel_id=1, source_target_pairs={{0,8},{1,9},{2,10},{3,11},{4,12},{5,13},{6,14},{7,15},{8,0},{9,1},... | collective-permute-start | bytes 442376 | tf_op jit(solution)/shard_map/ppermute | solution.py:42
  45.2 2.6 collective-permute-done.22
  55.1 2.5 collective-permute-done.12
  60.0 3.9 %collective-permute-done.23 = bf16[2,96,768]{2,1,0:T(8,128)(2,1)S(1)} collective-permute-done((bf16[2,96,768]{2,1,0:T(8,128)(2,1)S(1)}, bf16[2,96,768]{2,1,0:T(8,128)(2,1)S(1)}, u32[]{:S(2)}, u32[]{:S(2)}) %collective-permute-start.23) | collective-permute-done | bytes 294944 | tf_op jit(solution)/shard_map/ppermute | solution.py:42
  65.6 14.5 %collective-permute-done.5 = bf16[2,24,3200]{2,1,0:T(8,128)(2,1)S(1)} collective-permute-done((bf16[2,24,3200]{2,1,0:T(8,128)(2,1)S(1)}, bf16[2,24,3200]{2,1,0:T(8,128)(2,1)S(1)}, u32[]{:S(2)}, u32[]{:S(2)}) %collective-permute-start.5) | collective-permute-done | bytes 307232 | tf_op jit(solution)/shard_map/ppermute | solution.py:42
  84.3 12.1 %collective-permute-done.28.refs_3_ = bf16[2,2,96,768]{3,2,1,0:T(8,128)(2,1)S(1)} collective-permute-done((bf16[2,2,96,768]{3,2,1,0:T(8,128)(2,1)S(1)}, bf16[2,2,96,768]{3,2,1,0:T(8,128)(2,1)S(1)}, u32[]{:S(2)}, u32[]{:S(2)}) %collective-permute-start.28) | collective-permute-done | bytes 589856 | tf_op jit(solution)/shard_map/ppermute | solution.py:42
  98.5 10.5 %collective-permute-done.6.refs_3_ = bf16[2,2,24,3200]{3,2,1,0:T(8,128)(2,1)S(1)} collective-permute-done((bf16[2,2,24,3200]{3,2,1,0:T(8,128)(2,1)S(1)}, bf16[2,2,24,3200]{3,2,1,0:T(8,128)(2,1)S(1)}, u32[]{:S(2)}, u32[]{:S(2)}) %collective-permute-start.6) | collective-permute-done | bytes 614432 | tf_op jit(solution)/shard_map/ppermute | solution.py:42
  109.0 2.2 collective-permute-done.2.refs_1_
  114.5 4.8 %lay_out.4 = bf16[32,24,3072]{2,1,0:T(8,128)(2,1)} custom-call(s32[1]{0:T(128)} %bitcast.id_ref, bf16[2,2,24,3072]{3,2,1,0:T(8,128)(2,1)} %copy-done.4, bf16[2,2,24,3072]{3,2,1,0:T(8,128)(2,1)} %copy-done.13, bf16[2,2,24,3072]{3,2,1,0:T(8,128)(2,1)} %copy-done.3, bf16[2,2,24,3072]{3,2,1,0:T(8,128)(2,1)} %copy-done.11, bf16[2,2,24,3072]{3,2,1,0:T(8,128)(2,1)} %copy-done.15, ...), custom_call_target="tpu_custom_call" | custom-call | tf_op jit(solution)/shard_map/lay_out/pallas_call | solution.py:91
  119.4 4.9 %lay_out.5 = bf16[32,96,768]{2,1,0:T(8,128)(2,1)} custom-call(s32[1]{0:T(128)} %bitcast.id_ref, bf16[2,2,96,768]{3,2,1,0:T(8,128)(2,1)} %copy-done.6, bf16[2,2,96,768]{3,2,1,0:T(8,128)(2,1)} %collective-permute-done.24.refs_1_, bf16[2,2,96,768]{3,2,1,0:T(8,128)(2,1)} %copy-done.5, bf16[2,2,96,768]{3,2,1,0:T(8,128)(2,1)} %copy-done.14, ...), custom_call_target="tpu_custom_call" | custom-call | tf_op jit(solution)/shard_map/lay_out/pallas_call | solution.py:91
  124.3 4.9 %lay_out.3 = bf16[32,24,3200]{2,1,0:T(8,128)(2,1)} custom-call(s32[1]{0:T(128)} %bitcast.id_ref, bf16[2,2,24,3200]{3,2,1,0:T(8,128)(2,1)} %copy-done.1, bf16[2,2,24,3200]{3,2,1,0:T(8,128)(2,1)} %copy-done.9, bf16[2,2,24,3200]{3,2,1,0:T(8,128)(2,1)} %copy-done, bf16[2,2,24,3200]{3,2,1,0:T(8,128)(2,1)} %copy-done.8, ...), custom_call_target="tpu_custom_call" | custom-call | tf_op jit(solution)/shard_map/lay_out/pallas_call | solution.py:91
  129.2 3.5 %unpack_small.1 = (f32[8,768]{1,0:T(8,128)}, f32[1,3072]{1,0:T(1,128)}) custom-call(bf16[768,3200]{1,0:T(8,128)(2,1)} %bitcast.177), custom_call_target="tpu_custom_call" | custom-call | tf_op jit(solution)/shard_map/unpack_small/pallas_call | solution.py:194
  132.7 22.5 %attend.1 = (bf16[864,768]{1,0:T(8,128)(2,1)}, bf16[864,2304]{1,0:T(8,128)(2,1)}, bf16[864,768]{1,0:T(8,128)(2,1)}, f32[864,12]{1,0:T(8,128)}, f32[864,768]{1,0:T(8,128)}, /*index=5*/bf16[864,768]{1,0:T(8,128)(2,1)}) custom-call(bf16[864,768]{1,0:T(8,128)(2,1)} %bitcast.222, s32[3,1,288]{2,1,0:T(1,128)} %reshape.127.across_ref, s32[864,1]{1,0:T(8,128)} %reshape.163.down_ref, ...), custom_call_target="tpu_custom_call" | custom-call | flops 4841275392 | bytes 31457280 | tf_op jit(solution)/shard_map/attend/pallas_call | solution.py:315
  155.2 26.0 %feed_forward.1 = (bf16[864,768]{1,0:T(8,128)(2,1)}, bf16[864,3072]{1,0:T(8,128)(2,1)}, bf16[16,96,768]{2,1,0:T(8,128)(2,1)}, bf16[16,96,768]{2,1,0:T(8,128)(2,1)}, f32[1,3072]{1,0:T(1,128)}, /*index=5*/f32[8,768]{1,0:T(8,128)}) custom-call(s32[1]{0:T(128)} %bitcast.id_ref, bf16[864,768]{1,0:T(8,128)(2,1)} %get-tuple-element.40.second_ref, ...), custom_call_target="tpu_custom_call" | custom-call | flops 16307453952 | bytes 31457280 | tf_op jit(solution)/shard_map/feed_forward/pallas_call | solution.py:379
  181.7 18.3 %feed_back.1 = (f32[864,768]{1,0:T(8,128)}, bf16[16,24,3072]{2,1,0:T(8,128)(2,1)}, bf16[16,24,3072]{2,1,0:T(8,128)(2,1)}, f32[8,768]{1,0:T(8,128)}) custom-call(s32[1]{0:T(128)} %bitcast.id_ref, bf16[864,768]{1,0:T(8,128)(2,1)} %get-tuple-element.40.second_ref, bf16[864,3072]{1,0:T(8,128)(2,1)} %get-tuple-element.46.back_ref, bf16[864,768]{1,0:T(8,128)(2,1)} %bitcast.221, ...), custom_call_target="tpu_custom_call" | custom-call | flops 8153726976 | bytes 26214400 | tf_op jit(solution)/shard_map/feed_back/pallas_call | solution.py:454
  200.3 27.4 %attend_back.1 = (bf16[864,768]{1,0:T(8,128)(2,1)}, bf16[864,2304]{1,0:T(8,128)(2,1)}, bf16[864,768]{1,0:T(8,128)(2,1)}, f32[8,768]{1,0:T(8,128)}) custom-call(bf16[864,768]{1,0:T(8,128)(2,1)} %bitcast.223, s32[3,1,288]{2,1,0:T(1,128)} %reshape.127.across_ref, s32[864,1]{1,0:T(8,128)} %reshape.163.down_ref, bf16[768,3200]{1,0:T(8,128)(2,1)} %bitcast.179, ...), custom_call_target="tpu_custom_call" | custom-call | flops 5987893248 | bytes 26214400 | tf_op jit(solution)/shard_map/attend_back/pallas_call | solution.py:563
  227.7 16.3 %attend_weights.1 = (bf16[16,24,3200]{2,1,0:T(8,128)(2,1)}, bf16[16,24,3200]{2,1,0:T(8,128)(2,1)}) custom-call(s32[1]{0:T(128)} %bitcast.id_ref, bf16[864,768]{1,0:T(8,128)(2,1)} %get-tuple-element.49.first_ref, bf16[864,2304]{1,0:T(8,128)(2,1)} %get-tuple-element.50.dqkv_ref, bf16[864,768]{1,0:T(8,128)(2,1)} %get-tuple-element.51.ctx_ref, ...), custom_call_target="tpu_custom_call" | custom-call | flops 4076863488 | bytes 15728640 | tf_op jit(solution)/shard_map/attend_weights/pallas_call | solution.py:644
  244.2 3.1 add_convert_fusion.1
  255.5 8.2 %collective-permute-done.50 = bf16[2,2,96,768]{3,2,0,1:T(8,128)(2,1)S(1)} collective-permute-done((bf16[2,2,96,768]{3,2,0,1:T(8,128)(2,1)S(1)}, bf16[2,2,96,768]{3,2,0,1:T(8,128)(2,1)S(1)}, u32[]{:S(2)}, u32[]{:S(2)}) %collective-permute-start.50) | collective-permute-done | bytes 589856 | tf_op jit(solution)/shard_map/ppermute | solution.py:42
  267.0 9.3 %collective-permute-done.42 = bf16[2,2,24,3072]{3,2,0,1:T(8,128)(2,1)S(1)} collective-permute-done((bf16[2,2,24,3072]{3,2,0,1:T(8,128)(2,1)S(1)}, bf16[2,2,24,3072]{3,2,0,1:T(8,128)(2,1)S(1)}, u32[]{:S(2)}, u32[]{:S(2)}) %collective-permute-start.42) | collective-permute-done | bytes 589856 | tf_op jit(solution)/shard_map/ppermute | solution.py:42
  279.7 9.7 %collective-permute-done.34 = bf16[2,2,24,3200]{3,2,0,1:T(8,128)(2,1)S(1)} collective-permute-done((bf16[2,2,24,3200]{3,2,0,1:T(8,128)(2,1)S(1)}, bf16[2,2,24,3200]{3,2,0,1:T(8,128)(2,1)S(1)}, u32[]{:S(2)}, u32[]{:S(2)}) %collective-permute-start.34) | collective-permute-done | bytes 614432 | tf_op jit(solution)/shard_map/ppermute | solution.py:42
  293.0 4.5 %collective-permute-done.51 = bf16[2,96,768]{2,1,0:T(8,128)(2,1)S(1)} collective-permute-done((bf16[2,96,768]{2,1,0:T(8,128)(2,1)S(1)}, bf16[2,96,768]{2,1,0:T(8,128)(2,1)S(1)}, u32[]{:S(2)}, u32[]{:S(2)}) %collective-permute-start.51) | collective-permute-done | bytes 294944 | tf_op jit(solution)/shard_map/ppermute | solution.py:42
  300.4 3.3 collective-permute-done.43
  303.8 2.2 collective-permute-start.55
  308.0 3.2 collective-permute-start.47
  312.8 2.6 collective-permute-start.56
  315.4 9.9 %collective-permute-done.47 = bf16[24,3072]{1,0:T(8,128)(2,1)S(1)} collective-permute-done((bf16[24,3072]{1,0:T(8,128)(2,1)S(1)}, bf16[24,3072]{1,0:T(8,128)(2,1)S(1)}, u32[]{:S(2)}, u32[]{:S(2)}) %collective-permute-start.47) | collective-permute-done | bytes 147488 | tf_op jit(solution)/shard_map/ppermute | solution.py:42
  325.3 4.7 %collective-permute-start.39 = (bf16[24,3200]{1,0:T(8,128)(2,1)S(1)}, bf16[24,3200]{1,0:T(8,128)(2,1)S(1)}, u32[]{:S(2)}, u32[]{:S(2)}) collective-permute-start(bf16[24,3200]{1,0:T(8,128)(2,1)S(1)} %get-tuple-element.75), channel_id=1, source_target_pairs={{0,16},{1,17},{2,18},{3,19},{4,20},{5,21},{6,22},{7,23},{8,24},{9,... | collective-permute-start | bytes 460808 | tf_op jit(solution)/shard_map/ppermute | solution.py:42
  332.9 8.5 %collective-permute-done.39 = bf16[24,3200]{1,0:T(8,128)(2,1)S(1)} collective-permute-done((bf16[24,3200]{1,0:T(8,128)(2,1)S(1)}, bf16[24,3200]{1,0:T(8,128)(2,1)S(1)}, u32[]{:S(2)}, u32[]{:S(2)}) %collective-permute-start.39) | collective-permute-done | bytes 153632 | tf_op jit(solution)/shard_map/ppermute | solution.py:42
  (201 shorter events, 65.0 us)
Async XLA Ops:
  2.5 46.7 %collective-permute-start.3 = (bf16[24,3200]{1,0:T(8,128)(2,1)}, bf16[24,3200]{1,0:T(8,128)(2,1)S(1)}, u32[]{:S(2)}, u32[]{:S(2)}) collective-permute-start(bf16[24,3200]{1,0:T(8,128)(2,1)} %pack_near.1), channel_id=1, source_target_pairs={{0,16},{1,17},{2,18},{3,19},{4,20},{5,21},{6,22},{7,23},{8,24},{9,... | collective-permute-start | bytes 460808 | tf_op jit(solution)/shard_map/ppermute | solution.py:42
  6.6 44.3 %collective-permute-start.4 = (bf16[24,3200]{1,0:T(8,128)(2,1)}, bf16[24,3200]{1,0:T(8,128)(2,1)S(1)}, u32[]{:S(2)}, u32[]{:S(2)}) collective-permute-start(bf16[24,3200]{1,0:T(8,128)(2,1)} %pack_near.1), channel_id=1, source_target_pairs={{0,24},{1,25},{2,26},{3,27},{4,28},{5,29},{6,30},{7,31},{8,16},{9,... | collective-permute-start | bytes 460808 | tf_op jit(solution)/shard_map/ppermute | solution.py:42
  8.9 22.1 %collective-permute-start.14 = (bf16[24,3072]{1,0:T(8,128)(2,1)S(1)}, bf16[24,3072]{1,0:T(8,128)(2,1)S(1)}, u32[]{:S(2)}, u32[]{:S(2)}) collective-permute-start(bf16[24,3072]{1,0:T(8,128)(2,1)S(1)} %convert_element_type.222), channel_id=1, source_target_pairs={{0,16},{1,17},{2,18},{3,19},{4,20},{5,21},{6,22},{7,23},{8,24},{9,... | collective-permute-start | bytes 442376 | tf_op jit(solution)/shard_map/ppermute | solution.py:42
  10.7 20.4 %collective-permute-start.15 = (bf16[24,3072]{1,0:T(8,128)(2,1)S(1)}, bf16[24,3072]{1,0:T(8,128)(2,1)S(1)}, u32[]{:S(2)}, u32[]{:S(2)}) collective-permute-start(bf16[24,3072]{1,0:T(8,128)(2,1)S(1)} %convert_element_type.222), channel_id=1, source_target_pairs={{0,24},{1,25},{2,26},{3,27},{4,28},{5,29},{6,30},{7,31},{8,16},{9,... | collective-permute-start | bytes 442376 | tf_op jit(solution)/shard_map/ppermute | solution.py:42
  11.6 22.2 %collective-permute-start.11 = (bf16[24,3072]{1,0:T(8,128)(2,1)S(1)}, bf16[24,3072]{1,0:T(8,128)(2,1)S(1)}, u32[]{:S(2)}, u32[]{:S(2)}) collective-permute-start(bf16[24,3072]{1,0:T(8,128)(2,1)S(1)} %convert_element_type.222), channel_id=1, source_target_pairs={{0,8},{1,9},{2,10},{3,11},{4,12},{5,13},{6,14},{7,15},{8,0},{9,1},... | collective-permute-start | bytes 442376 | tf_op jit(solution)/shard_map/ppermute | solution.py:42
  53.6 28.2 %collective-permute-start.17 = (bf16[2,2,24,3072]{3,2,1,0:T(8,128)(2,1)S(1)}, bf16[2,2,24,3072]{3,2,1,0:T(8,128)(2,1)S(1)}, u32[]{:S(2)}, u32[]{:S(2)}) collective-permute-start(bf16[2,2,24,3072]{3,2,1,0:T(8,128)(2,1)S(1)} %pad_maximum_fusion.3.refs_2_), channel_id=1, source_target_pairs={{0,2},{1,3},{2,0},{3,1},{4,6},{5,7},{6,4},{7,5},{8,10},{9,11},{10,... | collective-permute-start | bytes 1769480 | tf_op jit(solution)/shard_map/ppermute | solution.py:42
  57.6 24.2 %collective-permute-start.20 = (bf16[2,2,24,3072]{3,2,1,0:T(8,128)(2,1)S(1)}, bf16[2,2,24,3072]{3,2,1,0:T(8,128)(2,1)S(1)}, u32[]{:S(2)}, u32[]{:S(2)}) collective-permute-start(bf16[2,2,24,3072]{3,2,1,0:T(8,128)(2,1)S(1)} %pad_maximum_fusion.3.refs_2_), channel_id=1, source_target_pairs={{0,1},{1,0},{2,3},{3,2},{4,5},{5,4},{6,7},{7,6},{8,9},{9,8},{10,11... | collective-permute-start | bytes 1769480 | tf_op jit(solution)/shard_map/ppermute | solution.py:42
  57.7 25.6 %collective-permute-start.13 = (bf16[2,2,24,3072]{3,2,1,0:T(8,128)(2,1)S(1)}, bf16[2,2,24,3072]{3,2,1,0:T(8,128)(2,1)S(1)}, u32[]{:S(2)}, u32[]{:S(2)}) collective-permute-start(bf16[2,2,24,3072]{3,2,1,0:T(8,128)(2,1)S(1)} %pad_maximum_fusion.2.refs_0_), channel_id=1, source_target_pairs={{0,4},{1,5},{2,6},{3,7},{4,0},{5,1},{6,2},{7,3},{8,12},{9,13},{10,... | collective-permute-start | bytes 1769480 | tf_op jit(solution)/shard_map/ppermute | solution.py:42
  59.3 20.7 %collective-permute-start.5 = (bf16[2,24,3200]{2,1,0:T(8,128)(2,1)S(1)}, bf16[2,24,3200]{2,1,0:T(8,128)(2,1)S(1)}, u32[]{:S(2)}, u32[]{:S(2)}) collective-permute-start(bf16[2,24,3200]{2,1,0:T(8,128)(2,1)S(1)} %get-tuple-element.78), channel_id=1, source_target_pairs={{0,4},{1,5},{2,6},{3,7},{4,0},{5,1},{6,2},{7,3},{8,12},{9,13},{10,... | collective-permute-start | bytes 921608 | tf_op jit(solution)/shard_map/ppermute | solution.py:42
  63.9 16.3 %collective-permute-start.1 = (bf16[2,24,3200]{2,1,0:T(8,128)(2,1)S(1)}, bf16[2,24,3200]{2,1,0:T(8,128)(2,1)S(1)}, u32[]{:S(2)}, u32[]{:S(2)}) collective-permute-start(bf16[2,24,3200]{2,1,0:T(8,128)(2,1)S(1)} %get-tuple-element.80), channel_id=1, source_target_pairs={{0,2},{1,3},{2,0},{3,1},{4,6},{5,7},{6,4},{7,5},{8,10},{9,11},{10,... | collective-permute-start | bytes 921608 | tf_op jit(solution)/shard_map/ppermute | solution.py:42
  80.2 16.2 %collective-permute-start.28 = (bf16[2,2,96,768]{3,2,1,0:T(8,128)(2,1)S(1)}, bf16[2,2,96,768]{3,2,1,0:T(8,128)(2,1)S(1)}, u32[]{:S(2)}, u32[]{:S(2)}) collective-permute-start(bf16[2,2,96,768]{3,2,1,0:T(8,128)(2,1)S(1)} %pad_maximum_fusion.5.refs_2_), channel_id=1, source_target_pairs={{0,2},{1,3},{2,0},{3,1},{4,6},{5,7},{6,4},{7,5},{8,10},{9,11},{10,... | collective-permute-start | bytes 1769480 | tf_op jit(solution)/shard_map/ppermute | solution.py:42
  81.7 16.2 %collective-permute-start.31 = (bf16[2,2,96,768]{3,2,1,0:T(8,128)(2,1)S(1)}, bf16[2,2,96,768]{3,2,1,0:T(8,128)(2,1)S(1)}, u32[]{:S(2)}, u32[]{:S(2)}) collective-permute-start(bf16[2,2,96,768]{3,2,1,0:T(8,128)(2,1)S(1)} %pad_maximum_fusion.5.refs_2_), channel_id=1, source_target_pairs={{0,1},{1,0},{2,3},{3,2},{4,5},{5,4},{6,7},{7,6},{8,9},{9,8},{10,11... | collective-permute-start | bytes 1769480 | tf_op jit(solution)/shard_map/ppermute | solution.py:42
  81.8 16.1 %collective-permute-start.24 = (bf16[2,2,96,768]{3,2,1,0:T(8,128)(2,1)S(1)}, bf16[2,2,96,768]{3,2,1,0:T(8,128)(2,1)}, u32[]{:S(2)}, u32[]{:S(2)}) collective-permute-start(bf16[2,2,96,768]{3,2,1,0:T(8,128)(2,1)S(1)} %pad_maximum_fusion.4.refs_0_), channel_id=1, source_target_pairs={{0,4},{1,5},{2,6},{3,7},{4,0},{5,1},{6,2},{7,3},{8,12},{9,13},{10,... | collective-permute-start | bytes 1769480 | tf_op jit(solution)/shard_map/ppermute | solution.py:42
  83.7 25.3 %collective-permute-start.6 = (bf16[2,2,24,3200]{3,2,1,0:T(8,128)(2,1)S(1)}, bf16[2,2,24,3200]{3,2,1,0:T(8,128)(2,1)S(1)}, u32[]{:S(2)}, u32[]{:S(2)}) collective-permute-start(bf16[2,2,24,3200]{3,2,1,0:T(8,128)(2,1)S(1)} %pad_maximum_fusion.1.refs_2_), channel_id=1, source_target_pairs={{0,2},{1,3},{2,0},{3,1},{4,6},{5,7},{6,4},{7,5},{8,10},{9,11},{10,... | collective-permute-start | bytes 1843208 | tf_op jit(solution)/shard_map/ppermute | solution.py:42
  181.2 62.9 %collective-permute-start.49 = (bf16[16,96,768]{2,1,0:T(8,128)(2,1)}, bf16[16,96,768]{2,1,0:T(8,128)(2,1)}, u32[]{:S(2)}, u32[]{:S(2)}) collective-permute-start(bf16[16,96,768]{2,1,0:T(8,128)(2,1)} %get-tuple-element.62), channel_id=1, source_target_pairs={{0,1},{1,0},{2,3},{3,2},{4,5},{5,4},{6,7},{7,6},{8,9},{9,8},{10,11... | collective-permute-start | bytes 7077896 | tf_op jit(solution)/shard_map/ppermute | solution.py:42
  200.0 50.6 %collective-permute-start.41 = (bf16[16,24,3072]{2,1,0:T(8,128)(2,1)}, bf16[16,24,3072]{2,1,0:T(8,128)(2,1)S(1)}, u32[]{:S(2)}, u32[]{:S(2)}) collective-permute-start(bf16[16,24,3072]{2,1,0:T(8,128)(2,1)} %get-tuple-element.60), channel_id=1, source_target_pairs={{0,1},{1,0},{2,3},{3,2},{4,5},{5,4},{6,7},{7,6},{8,9},{9,8},{10,11... | collective-permute-start | bytes 7077896 | tf_op jit(solution)/shard_map/ppermute | solution.py:42
  247.4 16.3 %collective-permute-start.50 = (bf16[2,2,96,768]{3,2,0,1:T(8,128)(2,1)S(1)}, bf16[2,2,96,768]{3,2,0,1:T(8,128)(2,1)S(1)}, u32[]{:S(2)}, u32[]{:S(2)}) collective-permute-start(bf16[2,2,96,768]{3,2,0,1:T(8,128)(2,1)S(1)} %bitcast.194), channel_id=1, source_target_pairs={{0,2},{1,3},{2,0},{3,1},{4,6},{5,7},{6,4},{7,5},{8,10},{9,11},{10,... | collective-permute-start | bytes 1769480 | tf_op jit(solution)/shard_map/ppermute | solution.py:42
  249.1 16.3 %collective-permute-start.53 = (bf16[2,2,96,768]{3,2,0,1:T(8,128)(2,1)S(1)}, bf16[2,2,96,768]{3,2,0,1:T(8,128)(2,1)S(1)}, u32[]{:S(2)}, u32[]{:S(2)}) collective-permute-start(bf16[2,2,96,768]{3,2,0,1:T(8,128)(2,1)S(1)} %bitcast.192), channel_id=1, source_target_pairs={{0,4},{1,5},{2,6},{3,7},{4,0},{5,1},{6,2},{7,3},{8,12},{9,13},{10,... | collective-permute-start | bytes 1769480 | tf_op jit(solution)/shard_map/ppermute | solution.py:42
  251.7 24.6 %collective-permute-start.42 = (bf16[2,2,24,3072]{3,2,0,1:T(8,128)(2,1)S(1)}, bf16[2,2,24,3072]{3,2,0,1:T(8,128)(2,1)S(1)}, u32[]{:S(2)}, u32[]{:S(2)}) collective-permute-start(bf16[2,2,24,3072]{3,2,0,1:T(8,128)(2,1)S(1)} %bitcast.195), channel_id=1, source_target_pairs={{0,2},{1,3},{2,0},{3,1},{4,6},{5,7},{6,4},{7,5},{8,10},{9,11},{10,... | collective-permute-start | bytes 1769480 | tf_op jit(solution)/shard_map/ppermute | solution.py:42
  252.4 25.5 %collective-permute-start.45 = (bf16[2,2,24,3072]{3,2,0,1:T(8,128)(2,1)S(1)}, bf16[2,2,24,3072]{3,2,0,1:T(8,128)(2,1)S(1)}, u32[]{:S(2)}, u32[]{:S(2)}) collective-permute-start(bf16[2,2,24,3072]{3,2,0,1:T(8,128)(2,1)S(1)} %bitcast.193), channel_id=1, source_target_pairs={{0,4},{1,5},{2,6},{3,7},{4,0},{5,1},{6,2},{7,3},{8,12},{9,13},{10,... | collective-permute-start | bytes 1769480 | tf_op jit(solution)/shard_map/ppermute | solution.py:42
  254.2 35.3 %collective-permute-start.34 = (bf16[2,2,24,3200]{3,2,0,1:T(8,128)(2,1)S(1)}, bf16[2,2,24,3200]{3,2,0,1:T(8,128)(2,1)S(1)}, u32[]{:S(2)}, u32[]{:S(2)}) collective-permute-start(bf16[2,2,24,3200]{3,2,0,1:T(8,128)(2,1)S(1)} %bitcast.191), channel_id=1, source_target_pairs={{0,2},{1,3},{2,0},{3,1},{4,6},{5,7},{6,4},{7,5},{8,10},{9,11},{10,... | collective-permute-start | bytes 1843208 | tf_op jit(solution)/shard_map/ppermute | solution.py:42
  263.7 27.5 %collective-permute-start.37 = (bf16[2,2,24,3200]{3,2,0,1:T(8,128)(2,1)S(1)}, bf16[2,2,24,3200]{3,2,0,1:T(8,128)(2,1)S(1)}, u32[]{:S(2)}, u32[]{:S(2)}) collective-permute-start(bf16[2,2,24,3200]{3,2,0,1:T(8,128)(2,1)S(1)} %bitcast.190), channel_id=1, source_target_pairs={{0,4},{1,5},{2,6},{3,7},{4,0},{5,1},{6,2},{7,3},{8,12},{9,13},{10,... | collective-permute-start | bytes 1843208 | tf_op jit(solution)/shard_map/ppermute | solution.py:42
  265.4 32.1 %collective-permute-start.51 = (bf16[2,96,768]{2,1,0:T(8,128)(2,1)S(1)}, bf16[2,96,768]{2,1,0:T(8,128)(2,1)S(1)}, u32[]{:S(2)}, u32[]{:S(2)}) collective-permute-start(bf16[2,96,768]{2,1,0:T(8,128)(2,1)S(1)} %slice_bitcast_fusion.6), channel_id=1, source_target_pairs={{0,4},{1,5},{2,6},{3,7},{4,0},{5,1},{6,2},{7,3},{8,12},{9,13},{10,... | collective-permute-start | bytes 884744 | tf_op jit(solution)/shard_map/ppermute | solution.py:42
  276.3 21.8 %collective-permute-start.54 = (bf16[2,96,768]{2,1,0:T(8,128)(2,1)S(1)}, bf16[2,96,768]{2,1,0:T(8,128)(2,1)S(1)}, u32[]{:S(2)}, u32[]{:S(2)}) collective-permute-start(bf16[2,96,768]{2,1,0:T(8,128)(2,1)S(1)} %slice_bitcast_fusion.4), channel_id=1, source_target_pairs={{0,2},{1,3},{2,0},{3,1},{4,6},{5,7},{6,4},{7,5},{8,10},{9,11},{10,... | collective-permute-start | bytes 884744 | tf_op jit(solution)/shard_map/ppermute | solution.py:42
  278.0 25.8 %collective-permute-start.43 = (bf16[2,24,3072]{2,1,0:T(8,128)(2,1)S(1)}, bf16[2,24,3072]{2,1,0:T(8,128)(2,1)S(1)}, u32[]{:S(2)}, u32[]{:S(2)}) collective-permute-start(bf16[2,24,3072]{2,1,0:T(8,128)(2,1)S(1)} %slice_bitcast_fusion.10), channel_id=1, source_target_pairs={{0,4},{1,5},{2,6},{3,7},{4,0},{5,1},{6,2},{7,3},{8,12},{9,13},{10,... | collective-permute-start | bytes 884744 | tf_op jit(solution)/shard_map/ppermute | solution.py:42
  289.5 16.7 %collective-permute-start.46 = (bf16[2,24,3072]{2,1,0:T(8,128)(2,1)S(1)}, bf16[2,24,3072]{2,1,0:T(8,128)(2,1)S(1)}, u32[]{:S(2)}, u32[]{:S(2)}) collective-permute-start(bf16[2,24,3072]{2,1,0:T(8,128)(2,1)S(1)} %slice_bitcast_fusion.8), channel_id=1, source_target_pairs={{0,2},{1,3},{2,0},{3,1},{4,6},{5,7},{6,4},{7,5},{8,10},{9,11},{10,... | collective-permute-start | bytes 884744 | tf_op jit(solution)/shard_map/ppermute | solution.py:42
  291.2 20.2 %collective-permute-start.35 = (bf16[2,24,3200]{2,1,0:T(8,128)(2,1)S(1)}, bf16[2,24,3200]{2,1,0:T(8,128)(2,1)S(1)}, u32[]{:S(2)}, u32[]{:S(2)}) collective-permute-start(bf16[2,24,3200]{2,1,0:T(8,128)(2,1)S(1)} %slice_bitcast_fusion.2), channel_id=1, source_target_pairs={{0,4},{1,5},{2,6},{3,7},{4,0},{5,1},{6,2},{7,3},{8,12},{9,13},{10,... | collective-permute-start | bytes 921608 | tf_op jit(solution)/shard_map/ppermute | solution.py:42
  298.1 32.7 %collective-permute-start.52 = (bf16[96,768]{1,0:T(8,128)(2,1)S(1)}, bf16[96,768]{1,0:T(8,128)(2,1)S(1)}, u32[]{:S(2)}, u32[]{:S(2)}) collective-permute-start(bf16[96,768]{1,0:T(8,128)(2,1)S(1)} %slice_bitcast_fusion.18), channel_id=1, source_target_pairs={{0,8},{1,9},{2,10},{3,11},{4,12},{5,13},{6,14},{7,15},{8,0},{9,1},... | collective-permute-start | bytes 442376 | tf_op jit(solution)/shard_map/ppermute | solution.py:42
  303.8 28.4 %collective-permute-start.55 = (bf16[96,768]{1,0:T(8,128)(2,1)S(1)}, bf16[96,768]{1,0:T(8,128)(2,1)S(1)}, u32[]{:S(2)}, u32[]{:S(2)}) collective-permute-start(bf16[96,768]{1,0:T(8,128)(2,1)S(1)} %get-tuple-element.81), channel_id=1, source_target_pairs={{0,16},{1,17},{2,18},{3,19},{4,20},{5,21},{6,22},{7,23},{8,24},{9,... | collective-permute-start | bytes 442376 | tf_op jit(solution)/shard_map/ppermute | solution.py:42
  308.0 17.3 %collective-permute-start.47 = (bf16[24,3072]{1,0:T(8,128)(2,1)S(1)}, bf16[24,3072]{1,0:T(8,128)(2,1)S(1)}, u32[]{:S(2)}, u32[]{:S(2)}) collective-permute-start(bf16[24,3072]{1,0:T(8,128)(2,1)S(1)} %get-tuple-element.83), channel_id=1, source_target_pairs={{0,16},{1,17},{2,18},{3,19},{4,20},{5,21},{6,22},{7,23},{8,24},{9,... | collective-permute-start | bytes 442376 | tf_op jit(solution)/shard_map/ppermute | solution.py:42
  312.8 19.3 %collective-permute-start.56 = (bf16[96,768]{1,0:T(8,128)(2,1)S(1)}, bf16[96,768]{1,0:T(8,128)(2,1)S(1)}, u32[]{:S(2)}, u32[]{:S(2)}) collective-permute-start(bf16[96,768]{1,0:T(8,128)(2,1)S(1)} %get-tuple-element.82), channel_id=1, source_target_pairs={{0,24},{1,25},{2,26},{3,27},{4,28},{5,29},{6,30},{7,31},{8,16},{9,... | collective-permute-start | bytes 442376 | tf_op jit(solution)/shard_map/ppermute | solution.py:42
  325.3 16.2 %collective-permute-start.39 = (bf16[24,3200]{1,0:T(8,128)(2,1)S(1)}, bf16[24,3200]{1,0:T(8,128)(2,1)S(1)}, u32[]{:S(2)}, u32[]{:S(2)}) collective-permute-start(bf16[24,3200]{1,0:T(8,128)(2,1)S(1)} %get-tuple-element.75), channel_id=1, source_target_pairs={{0,16},{1,17},{2,18},{3,19},{4,20},{5,21},{6,22},{7,23},{8,24},{9,... | collective-permute-start | bytes 460808 | tf_op jit(solution)/shard_map/ppermute | solution.py:42
  (47 other events, 792.8 us)
